TPU v7x, 128 devices: a whole 4x4x4 slice. The times are simulated.
128 devices in a mesh: dp: 4 (over z), ctx: 32 (over y, x, core).
Axes of the slice: x: 4, y: 4, z: 4, core: 2. Of those that a mesh axis runs over, the one named last changes fastest.
Arguments:
- source_picture_sequence: bfloat16 [4, 128, 8, 8, 16, 128], P('dp', 'ctx'), may hold values from -6 to 6
- slot_assignment: int32 [128], replicated, may hold values from 0 to 127, as said below
- segment_piece_counts: int32 [16], replicated, may hold values from 1 to 16, 128 in all
- logit_scaling: float32 [4], replicated, may hold values from 1 to 16
- filter_tap_coefficients: bfloat16 [3456, 256], replicated, may hold values from -0.109375 to 0.109375
- triple_linear_matrix: bfloat16 [256, 768], replicated, may hold values from -0.375 to 0.375
- final_linear_matrix: bfloat16 [256, 256], replicated, may hold values from -0.375 to 0.375
- upstream_gradient: bfloat16 [4, 128, 4, 128, 256], P('dp', 'ctx'), may hold values from -6 to 6
Outputs:
- latents: bfloat16 [4, 128, 4, 128, 256], P('dp', 'ctx')
- conv_grad: float32 [3456, 256], P('ctx')
Inputs may be any that keep to these rules, and one draw needn't show every extreme that they name: `slot_assignment`: A permutation of the span numbers; entry i names the span at slot i, held by device i // 4. Each quarter of the span numbers, in order, fills one of the 4 positions on every device. The spans that follow one device's spans lie on at most two devices, at most two on any one device, and so do the spans that precede them; in every draw some device has two spans followed by spans on one other device.
All inputs are finite; a program needn't handle non-finite values.
Results may differ from a plain program's by a relative error of at most 0.0058.
Values may be sent and summed in bfloat16 or wider, within the bound.
A program may use at most 128 MiB of HBM per device.

v0:
```python
import jax
import jax.numpy as jnp
from jax import lax
from jax.sharding import PartitionSpec as P

masked_score = -1e30


def clip_marks(segment_piece_counts, span_ids):
    clip_ends = jnp.cumsum(segment_piece_counts, dtype=jnp.int32)
    clip_starts = clip_ends - segment_piece_counts
    clip_index = jnp.sum(
        (span_ids[:, None] >= clip_ends[None, :]).astype(jnp.int32), axis=1, dtype=jnp.int32
    )
    opening = jnp.any(span_ids[:, None] == clip_starts[None, :], axis=1)
    return (clip_index, opening)


def locate(span_ids, slot_assignment):
    slot_ids = jnp.arange(slot_assignment.shape[0], dtype=jnp.int32)
    matches = slot_assignment[None, :] == span_ids[:, None]
    return jnp.sum(jnp.where(matches, slot_ids[None, :], 0), axis=1, dtype=jnp.int32)


def conv_patches(frames):
    span_total, unused_len, rows_h, cols_w, channel_in = frames.shape
    padded = jnp.pad(frames, ((0, 0), (0, 0), (1, 1), (1, 1), (0, 0)))
    tap_list = []
    for step_t in range(3):
        for step_h in range(3):
            for step_w in range(3):
                tap_list.append(
                    padded[
                        :,
                        step_t : step_t + 7 : 2,
                        step_h : step_h + rows_h,
                        step_w : step_w + cols_w,
                        :,
                    ]
                )
    return jnp.concatenate(tap_list, axis=-1).reshape(-1, 27 * channel_in)


def timewise_softmax_mixing(
    grid_tile_entries, logit_scaling, triple_linear_matrix, final_linear_matrix, allowance_pattern
):
    channel_width = grid_tile_entries.shape[-1]
    channel_group_index = logit_scaling.shape[0]
    head_size = channel_width // channel_group_index
    values32 = grid_tile_entries.astype(jnp.float32)
    normed = (
        values32 * lax.rsqrt(jnp.mean(values32 * values32, axis=-1, keepdims=True) + 1e-06)
    ).astype(jnp.bfloat16)
    projected = jnp.einsum(
        "gac,cd->gad", normed, triple_linear_matrix, preferred_element_type=jnp.float32
    )
    head_shape = grid_tile_entries.shape[:2] + (channel_group_index, head_size)
    queries = projected[..., :channel_width].reshape(head_shape)
    keys_all = projected[..., channel_width : 2 * channel_width].reshape(head_shape)
    head_values = projected[..., 2 * channel_width :].reshape(head_shape).astype(jnp.bfloat16)
    queries = queries * lax.rsqrt(jnp.sum(queries * queries, axis=-1, keepdims=True) + 1e-06)
    keys_all = keys_all * lax.rsqrt(jnp.sum(keys_all * keys_all, axis=-1, keepdims=True) + 1e-06)
    affinity_logits = jnp.einsum(
        "gahd,gbhd->ghab", queries, keys_all, precision=lax.Precision.HIGHEST
    )
    affinity_logits = affinity_logits * logit_scaling[None, :, None, None]
    affinity_logits = jnp.where(allowance_pattern[None, None], affinity_logits, masked_score)
    highest = jnp.max(affinity_logits, axis=-1, keepdims=True)
    weights = jnp.exp(affinity_logits - highest)
    probabilities = (weights / jnp.sum(weights, axis=-1, keepdims=True)).astype(jnp.bfloat16)
    mixed_heads = jnp.einsum(
        "ghab,gbhd->gahd", probabilities, head_values, preferred_element_type=jnp.float32
    )
    mixed_heads = mixed_heads.astype(jnp.bfloat16).reshape(grid_tile_entries.shape)
    branch = jnp.einsum(
        "gac,cd->gad", mixed_heads, final_linear_matrix, preferred_element_type=jnp.float32
    )
    return (values32 + branch).astype(jnp.bfloat16)


def per_device(
    source_picture_sequence,
    slot_assignment,
    segment_piece_counts,
    logit_scaling,
    filter_tap_coefficients,
    triple_linear_matrix,
    final_linear_matrix,
    upstream_gradient,
):
    my_index = lax.axis_index("ctx")
    local_frames = source_picture_sequence[0]
    slot_count = local_frames.shape[0]
    my_spans = lax.dynamic_slice_in_dim(slot_assignment, my_index * slot_count, slot_count)
    unused_clip, opening = clip_marks(segment_piece_counts, my_spans)
    pred_slot = locate(jnp.maximum(my_spans - 1, 0), slot_assignment)
    tails = local_frames[:, 6:]
    shard_rows = lax.all_gather(tails, "ctx", axis=0, tiled=True)
    inside = (pred_slot >= 0) & (pred_slot < shard_rows.shape[0])
    chosen = shard_rows[jnp.clip(pred_slot, 0, shard_rows.shape[0] - 1)]
    previous = jnp.where(inside[:, None, None, None, None], chosen, jnp.zeros_like(tails))
    previous = jnp.where(opening[:, None, None, None, None], jnp.zeros_like(previous), previous)
    patches = conv_patches(jnp.concatenate([previous, local_frames], axis=1))
    channels = filter_tap_coefficients.shape[1]
    cell_count = local_frames.shape[2] * local_frames.shape[3]
    conv_out = jnp.dot(patches, filter_tap_coefficients, preferred_element_type=jnp.float32).astype(
        jnp.bfloat16
    )
    conv_out = conv_out.reshape(slot_count, 4, cell_count, channels)
    grad_rows = upstream_gradient[0].reshape(-1, channels)
    grad_share = lax.psum_scatter(
        jnp.dot(patches.T, grad_rows, preferred_element_type=jnp.float32),
        "ctx",
        scatter_dimension=0,
        tiled=True,
    )
    conv_grad = lax.psum(grad_share, "dp")
    gathered = lax.all_to_all(conv_out, "ctx", split_axis=2, concat_axis=0, tiled=True)
    frame_total = gathered.shape[0] * 4
    cells_dev = gathered.shape[2]
    location_entry_count = jnp.transpose(
        gathered.reshape(frame_total, cells_dev, channels), (1, 0, 2)
    )
    clip_all, unused_open = clip_marks(segment_piece_counts, slot_assignment)
    frame_clip = jnp.repeat(clip_all, 4)
    frame_time = (slot_assignment[:, None] * 4 + jnp.arange(4, dtype=jnp.int32)[None, :]).reshape(
        -1
    )
    allowance_pattern = (frame_clip[:, None] == frame_clip[None, :]) & (
        frame_time[None, :] <= frame_time[:, None]
    )
    cell_group = 1
    block_list = location_entry_count.reshape(
        cells_dev // cell_group, cell_group, frame_total, channels
    )
    blended_result = lax.map(
        lambda grid_tile_entries: timewise_softmax_mixing(
            grid_tile_entries,
            logit_scaling,
            triple_linear_matrix,
            final_linear_matrix,
            allowance_pattern,
        ),
        block_list,
    )
    blended_result = jnp.transpose(
        blended_result.reshape(cells_dev, frame_total, channels), (1, 0, 2)
    ).reshape(gathered.shape)
    latents = lax.all_to_all(blended_result, "ctx", split_axis=0, concat_axis=2, tiled=True)
    return (latents[None], conv_grad)


def solution(mesh):
    placed = (
        P("dp", "ctx", None, None, None, None),
        P(),
        P(),
        P(),
        P(),
        P(),
        P(),
        P("dp", "ctx", None, None, None),
    )
    return jax.shard_map(
        per_device,
        mesh=mesh,
        in_specs=placed,
        out_specs=(P("dp", "ctx", None, None, None), P("ctx", None)),
        check_vma=False,
    )
```

profile of v0, /device:TPU:1, one launch (start us, length us, event | category | flops | bytes accessed | tf_op | source)
XLA Modules:
  0.0 375.3 jit_solution(8046809622749582942)
XLA Ops:
  14.2 52.3 %all-gather.2.cloned.1.call-done = bf16[128,2,8,16,128]{4,3,2,1,0:T(8,128)(2,1)} async-done(((bf16[4,2,8,16,128]{4,3,2,1,0:T(8,128)(2,1)}), bf16[128,2,8,16,128]{4,3,2,1,0:T(8,128)(2,1)}) %all-gather.2.cloned.1.call-update) | async-done | bytes 8388624 | tf_op jit(solution)/shard_map/all_gather | solution.py:98
  66.5 4.0 %gather_fusion = bf16[4,2,8,16,128]{4,3,2,1,0:T(8,128)(2,1)S(1)} fusion(bf16[128,2,8,16,128]{4,3,2,1,0:T(8,128)(2,1)} %all-gather.2.cloned.1.call-done, s32[1024]{0:T(1024)S(1)} %pad_clamp_fusion), kind=kCustom, calls=%fused_computation | custom fusion | bytes 524304 | tf_op jit(solution)/shard_map/gather | solution.py:100
  79.6 4.1 %convolution_convert_fusion = bf16[2048,256]{1,0:T(8,128)(2,1)S(1)} fusion(bf16[2048,3456]{1,0:T(8,128)(2,1)S(1)} %bitcast.102, bf16[3456,256]{1,0:T(8,128)(2,1)S(1)} %copy-done), kind=kOutput, calls=%fused_computation.47 | convolution fusion | flops 3624402944 | bytes 16973824 | tf_op jit(solution)/shard_map/dot_general | solution.py:106
  86.4 5.5 %all-to-all-start = ((bf16[4,4,128,256]{3,1,0,2:T(4,128)(2,1)}), bf16[4,4,128,256]{3,1,0,2:T(4,128)(2,1)S(1)}, u32[]{:S(2)}, u32[]{:S(2)}) async-start(bf16[4,4,128,256]{3,1,0,2:T(4,128)(2,1)} %copy.55), calls=%async_computation | async-start | bytes 2097152 | tf_op jit(solution)/shard_map/all_to_all | solution.py:118
  92.0 10.9 %fusion.36 = f32[3456,256]{1,0:T(8,128)} fusion(bf16[2048,3456]{1,0:T(8,128)(2,1)} %bitcast.103, bf16[2048,256]{1,0:T(8,128)(2,1)} %bitcast.105), kind=kOutput, calls=%fused_computation.91 | convolution fusion | flops 3623878656 | bytes 18743296 | tf_op jit(solution)/shard_map/dot_general | solution.py:112
  102.9 6.1 %all-to-all-done = bf16[4,4,128,256]{3,1,0,2:T(4,128)(2,1)S(1)} async-done(((bf16[4,4,128,256]{3,1,0,2:T(4,128)(2,1)}), bf16[4,4,128,256]{3,1,0,2:T(4,128)(2,1)S(1)}, u32[]{:S(2)}, u32[]{:S(2)}) %all-to-all-start) | async-done | bytes 1048608 | tf_op jit(solution)/shard_map/all_to_all | solution.py:118
  110.4 2.1 reshape.266
  112.5 120.4 %while.11 = (s32[]{:T(128)}, bf16[4,1,512,256]{3,2,1,0:T(8,128)(2,1)}, bf16[4,1,512,256]{3,2,1,0:T(8,128)(2,1)}, bf16[256,768]{1,0:T(8,128)(2,1)}, f32[4]{0:T(12...) while((s32[]{:T(128)}, ...), condition=%wide.region_10.11_spmd.clone, body=%wide.region_4.10_spmd.clone.sunk | while | flops 1219232768 | bytes 31814784 | solution.py:136
  127.0 4.7 %fusion.65 = f32[4,512,512]{1,2,0:T(8,128)S(1)} fusion(f32[512,4,64]{0,2,1:T(8,128)} %bitcast.89, f32[512,4,64]{0,2,1:T(8,128)} %bitcast.90, f32[512,4]{0,1:T(4,128)S(1)} %get-tuple-element.153, f32[512,4]{0,1:T(4,128)S(1)} %get-tuple-element.154), kind=kOutput, calls=%fused_computation.24.clone.1 | convolution fusion | flops 805568512 | bytes 5259264 | tf_op jit(solution)/shard_map/while/body/eval_jaxpr/gahd,gbhd->ghab/dot_general | solution.py:63
  132.0 4.2 %fusion.66 = (f32[4,512]{1,0:T(4,128)S(1)}, f32[4,512,512]{1,2,0:T(8,128)}) fusion(f32[4,512,512]{1,2,0:T(8,128)S(1)} %fusion.65, f32[4]{0:T(128)S(1)} %get-tuple-element.181, pred[512,512]{0,1:T(8,128)(4,1)S(1)} %compare_and_fusion.3), kind=kOutput, calls=%fused_computation.90.clone.1 | output fusion | flops 6291967 | bytes 8658960 | tf_op jit(solution)/shard_map/while/body/eval_jaxpr/sub | solution.py:69
  138.0 2.7 fusion.67
  157.1 4.7 %fusion.65 = f32[4,512,512]{1,2,0:T(8,128)S(1)} fusion(f32[512,4,64]{0,2,1:T(8,128)} %bitcast.89, f32[512,4,64]{0,2,1:T(8,128)} %bitcast.90, f32[512,4]{0,1:T(4,128)S(1)} %get-tuple-element.153, f32[512,4]{0,1:T(4,128)S(1)} %get-tuple-element.154), kind=kOutput, calls=%fused_computation.24.clone.1 | convolution fusion | flops 805568512 | bytes 5259264 | tf_op jit(solution)/shard_map/while/body/eval_jaxpr/gahd,gbhd->ghab/dot_general | solution.py:63
  162.1 4.2 %fusion.66 = (f32[4,512]{1,0:T(4,128)S(1)}, f32[4,512,512]{1,2,0:T(8,128)}) fusion(f32[4,512,512]{1,2,0:T(8,128)S(1)} %fusion.65, f32[4]{0:T(128)S(1)} %get-tuple-element.181, pred[512,512]{0,1:T(8,128)(4,1)S(1)} %compare_and_fusion.3), kind=kOutput, calls=%fused_computation.90.clone.1 | output fusion | flops 6291967 | bytes 8658960 | tf_op jit(solution)/shard_map/while/body/eval_jaxpr/sub | solution.py:69
  168.1 2.7 fusion.67
  187.2 4.7 %fusion.65 = f32[4,512,512]{1,2,0:T(8,128)S(1)} fusion(f32[512,4,64]{0,2,1:T(8,128)} %bitcast.89, f32[512,4,64]{0,2,1:T(8,128)} %bitcast.90, f32[512,4]{0,1:T(4,128)S(1)} %get-tuple-element.153, f32[512,4]{0,1:T(4,128)S(1)} %get-tuple-element.154), kind=kOutput, calls=%fused_computation.24.clone.1 | convolution fusion | flops 805568512 | bytes 5259264 | tf_op jit(solution)/shard_map/while/body/eval_jaxpr/gahd,gbhd->ghab/dot_general | solution.py:63
  192.2 4.2 %fusion.66 = (f32[4,512]{1,0:T(4,128)S(1)}, f32[4,512,512]{1,2,0:T(8,128)}) fusion(f32[4,512,512]{1,2,0:T(8,128)S(1)} %fusion.65, f32[4]{0:T(128)S(1)} %get-tuple-element.181, pred[512,512]{0,1:T(8,128)(4,1)S(1)} %compare_and_fusion.3), kind=kOutput, calls=%fused_computation.90.clone.1 | output fusion | flops 6291967 | bytes 8658960 | tf_op jit(solution)/shard_map/while/body/eval_jaxpr/sub | solution.py:69
  198.2 2.7 fusion.67
  217.3 4.7 %fusion.65 = f32[4,512,512]{1,2,0:T(8,128)S(1)} fusion(f32[512,4,64]{0,2,1:T(8,128)} %bitcast.89, f32[512,4,64]{0,2,1:T(8,128)} %bitcast.90, f32[512,4]{0,1:T(4,128)S(1)} %get-tuple-element.153, f32[512,4]{0,1:T(4,128)S(1)} %get-tuple-element.154), kind=kOutput, calls=%fused_computation.24.clone.1 | convolution fusion | flops 805568512 | bytes 5259264 | tf_op jit(solution)/shard_map/while/body/eval_jaxpr/gahd,gbhd->ghab/dot_general | solution.py:63
  222.3 4.2 %fusion.66 = (f32[4,512]{1,0:T(4,128)S(1)}, f32[4,512,512]{1,2,0:T(8,128)}) fusion(f32[4,512,512]{1,2,0:T(8,128)S(1)} %fusion.65, f32[4]{0:T(128)S(1)} %get-tuple-element.181, pred[512,512]{0,1:T(8,128)(4,1)S(1)} %compare_and_fusion.3), kind=kOutput, calls=%fused_computation.90.clone.1 | output fusion | flops 6291967 | bytes 8658960 | tf_op jit(solution)/shard_map/while/body/eval_jaxpr/sub | solution.py:69
  228.3 2.7 fusion.67
  232.9 3.0 copy.61
  235.9 4.0 %all-to-all-start.1 = ((bf16[128,4,4,256]{3,2,1,0:T(4,128)(2,1)}), bf16[128,4,4,256]{3,2,1,0:T(4,128)(2,1)S(1)}, u32[]{:S(2)}, u32[]{:S(2)}) async-start(bf16[128,4,4,256]{3,2,1,0:T(4,128)(2,1)} %bitcast.95), calls=%async_computation.1 | async-start | bytes 2097152 | tf_op jit(solution)/shard_map/all_to_all | solution.py:149
  240.0 83.0 %fusion.2 = f32[112,256]{1,0:T(8,128)S(1)} fusion(f32[3456,256]{1,0:T(8,128)} %fusion.36), kind=kCustom, calls=%all-reduce-scatter | all-reduce-scatter fusion | flops 917505 | bytes 3654144
  330.2 36.7 %all-reduce.5.cloned.1.call-done = f32[108,256]{1,0:T(8,128)} async-done(((f32[108,256]{1,0:T(8,128)}), f32[108,256]{1,0:T(8,128)}) %all-reduce.5.cloned.1.call-update) | async-done | bytes 110608 | tf_op jit(solution)/shard_map/psum | solution.py:117
  (135 shorter events, 102.0 us)
Async XLA Ops:
  7.2 72.4 %copy-start = (bf16[3456,256]{1,0:T(8,128)(2,1)S(1)}, bf16[3456,256]{1,0:T(8,128)(2,1)}, u32[]{:S(2)}) copy-start(bf16[3456,256]{1,0:T(8,128)(2,1)} %param.14) | copy-start | bytes 5308420
  7.2 59.4 %all-gather.2.cloned.1.call-start = ((), (), s32[]{:S(2)}) async-start(), calls=%async_computation.2 | async-start | bytes 8650752 | tf_op jit(solution)/shard_map/all_gather | solution.py:98
  79.6 5.1 %copy-start.1 = (bf16[4,4,8,16,3456]{4,3,2,1,0:T(8,128)(2,1)}, bf16[4,4,8,16,3456]{4,3,2,1,0:T(8,128)(2,1)S(1)}, u32[]{:S(2)}) copy-start(bf16[4,4,8,16,3456]{4,3,2,1,0:T(8,128)(2,1)S(1)} %slice_dynamic-update-slice_fusion) | copy-start | bytes 42467332
  86.4 22.5 %all-to-all-start = ((bf16[4,4,128,256]{3,1,0,2:T(4,128)(2,1)}), bf16[4,4,128,256]{3,1,0,2:T(4,128)(2,1)S(1)}, u32[]{:S(2)}, u32[]{:S(2)}) async-start(bf16[4,4,128,256]{3,1,0,2:T(4,128)(2,1)} %copy.55), calls=%async_computation | async-start | bytes 2097152 | tf_op jit(solution)/shard_map/all_to_all | solution.py:118
  91.9 20.6 %copy-start.3 = (bf16[256,256]{1,0:T(8,128)(2,1)S(1)}, bf16[256,256]{1,0:T(8,128)(2,1)}, u32[]{:S(2)}) copy-start(bf16[256,256]{1,0:T(8,128)(2,1)} %param.16) | copy-start | bytes 393220
  92.0 20.6 %copy-start.4 = (f32[4]{0:T(128)S(1)}, f32[4]{0:T(128)}, u32[]{:S(2)}) copy-start(f32[4]{0:T(128)} %param.13) | copy-start | bytes 52
  112.5 213.7 %copy-start.2 = (u32[128]{0:T(128)S(1)}, u32[128]{0:T(128)}, u32[]{:S(2)}) copy-start(u32[128]{0:T(128)} %constant.55) | copy-start | bytes 1540
  235.9 92.7 %all-to-all-start.1 = ((bf16[128,4,4,256]{3,2,1,0:T(4,128)(2,1)}), bf16[128,4,4,256]{3,2,1,0:T(4,128)(2,1)S(1)}, u32[]{:S(2)}, u32[]{:S(2)}) async-start(bf16[128,4,4,256]{3,2,1,0:T(4,128)(2,1)} %bitcast.95), calls=%async_computation.1 | async-start | bytes 2097152 | tf_op jit(solution)/shard_map/all_to_all | solution.py:149
  239.9 127.0 %all-reduce.5.cloned.1.call-start = ((), (), s32[]{:S(2)}) async-start(), calls=%async_computation.3 | async-start | bytes 229376 | tf_op jit(solution)/shard_map/psum | solution.py:117
  322.9 4.5 %collective-permute-start = (f32[112,256]{1,0:T(8,128)S(1)}, f32[112,256]{1,0:T(8,128)S(1)}, u32[]{:S(2)}, u32[]{:S(2)}) collective-permute-start(f32[112,256]{1,0:T(8,128)S(1)} %fusion.2), channel_id=1, source_target_pairs={{0,1},{1,2},{2,3},{3,4},{4,5},{5,6},{6,7},{7,8},{8,9},{9,10},{10,1... | collective-permute-start | bytes 344072
  324.9 2.5 collective-permute-start.1
Sparse Core Ops, SparseCore 0:
  10.3 56.2 all-gather.1
  328.7 38.1 all-reduce.4
where the time goes:
time: 379 us; the launch traced here: 375 us
  waiting for transfers between devices  95.2 us (25%)
  blocking collectives  83 us (22%)
  local copies, waits for them, and re-layouts  67.8 us (18%)
  matrix products  58.3 us (15%)
  other arithmetic  42.9 us (11%)
  between operations  15.1 us (4%)
  starting transfers between devices  12.8 us (3%)
    unnamed x1, blocking collectives  83 us
    all_gather x1, waiting for transfers between devices, per_device(): shard_rows = lax.all_gather(tails, 'ctx', axis=0, tiled=True)  52.3 us
    psum x1, waiting for transfers between devices, per_device(): conv_grad = lax.psum(grad_share, 'dp')  36.7 us
    dot_general x4, matrix products, timewise_softmax_mixing(): jnp.einsum('gahd,gbhd->ghab', queries, keys_all, precision=lax.Precision....  18.9 us
    sub x4, other arithmetic, timewise_softmax_mixing(): weights = jnp.exp(affinity_logits - highest)  16.6 us
    unnamed x42, local copies, waits for them, and re-layouts  11.7 us
    dot_general x1, matrix products, per_device(): jnp.dot(patches.T, grad_rows, preferred_element_type=jnp.float32)  10.9 us
    dot_general x4, matrix products, timewise_softmax_mixing(): jnp.einsum('ghab,gbhd->gahd', probabilities, head_values, preferred_eleme...  10.7 us
  transfers between devices with their start and end apart: 6, of which 3 were waited for; matrix products, arithmetic and copies ran while one was open for 27% of the time, Pallas kernels for 0%

commit v1 on v0

v1 whole, which is shorter than its diff:
```python
import jax
import jax.numpy as jnp
import numpy as np
from jax import lax
from jax.experimental import pallas as pl
from jax.experimental.pallas import tpu as pltpu
from jax.sharding import PartitionSpec as P

BF = jnp.bfloat16
F32 = jnp.float32
MESH = pl.DeviceIdType.MESH
DEV = 32
LOG2E = 1.4426950408889634


def one_hot_rows(rows, cols, pairs):
    table = np.zeros((rows, cols), np.float32)
    for row, col in pairs:
        table[row, col] = 1.0
    return jnp.asarray(table, BF)


def frame_rows():
    pairs = []
    for r in range(4):
        for qp in range(-1, 5):
            for k in range(4):
                for s in range(4):
                    q = qp + 4 * k
                    if 0 <= q < 16:
                        pairs.append((((r * 6 + qp + 1) * 4 + k) * 4 + s, (r * 4 + s) * 16 + q))
    return one_hot_rows(384, 256, pairs)


def gradient_rows():
    pairs = []
    for r in range(4):
        for qp in range(4):
            for k in range(4):
                for s in range(4):
                    pairs.append((((r * 4 + qp) * 4 + k) * 4 + s, (r * 4 + s) * 16 + qp + 4 * k))
    return one_hot_rows(256, 256, pairs)


def result_rows():
    pairs = []
    for qp in range(4):
        for k in range(4):
            for t in range(4):
                for s in range(4):
                    pairs.append(((s * 4 + t) * 16 + qp + 4 * k, ((qp * 4 + k) * 4 + t) * 4 + s))
    return one_hot_rows(256, 256, pairs)


def column_shifts():
    pairs = []
    for r in range(8):
        for k in range(4):
            for s in range(4):
                if k < 3:
                    pairs.append(((r * 4 + k) * 4 + s, (r * 4 + k + 1) * 4 + s))
                if k > 0:
                    pairs.append((128 + (r * 4 + k) * 4 + s, (r * 4 + k - 1) * 4 + s))
    return one_hot_rows(256, 128, pairs)


def slot_expand():
    pairs = []
    for e in range(32):
        for k in range(4):
            for s in range(4):
                pairs.append((4 * e + s, (e * 4 + k) * 4 + s))
    return one_hot_rows(128, 512, pairs)


def head_sums():
    table = np.kron(np.eye(4), np.ones((64, 64)))
    return jnp.asarray(table, BF)


def mm(a, b):
    return jnp.dot(a, b, preferred_element_type=F32)


def section_kernel(
    x_ref, w_ref, wqkv_ref, wout_ref, ug_ref, sa_ref, cnt_ref, scale_ref,
    px_ref, pg_ref, po_ref, sh_ref, ex_ref, hs_ref,
    out_ref, cg_ref,
    xp, xt, pat, t1r, t2s, t2r, cs, cr, gt, dw, gf, gbs, r1, s1b, acc1, r2, s2b, acc2, r3, s3b, acc3, r4, s4, r5,
    hot_t, hot_s, hot_u, mask, ys, qs, ks, vs, osb, rb, orv,
    send_sem, recv_sem, red_send, red_recv,
):
    z = lax.axis_index("dp")
    me = lax.axis_index("ctx")
    core = me % 2
    chip_x = (me // 2) % 4
    chip_y = me // 8

    barrier = pltpu.get_barrier_semaphore()

    def greet(step, carry):
        peer = (me + step) % DEV
        pl.semaphore_signal(barrier, inc=1, device_id={"ctx": peer}, device_id_type=MESH)
        return carry

    lax.fori_loop(1, DEV, greet, 0)
    for dz in range(1, 4):
        pl.semaphore_signal(barrier, inc=1, device_id={"dp": (z + dz) % 4}, device_id_type=MESH)

    def spread(source, target, phase):
        def one(step, carry):
            peer = (me + step) % DEV
            pltpu.make_async_remote_copy(
                src_ref=source(peer), dst_ref=target(me), send_sem=send_sem.at[phase],
                recv_sem=recv_sem.at[phase], device_id={"ctx": peer}, device_id_type=MESH,
            ).start()
            return carry

        lax.fori_loop(1, DEV, one, 0)

    def landed(view, phase):
        pltpu.make_async_copy(view, view, recv_sem.at[phase]).wait()

    def left(view, phase):
        pltpu.make_async_copy(view, view, send_sem.at[phase]).wait()

    zero_rows = jnp.zeros((8, 6, 16, 128), BF)
    xp[:, 0] = zero_rows
    xp[:, 9] = zero_rows
    xt[:, 0] = zero_rows[:2]
    xt[:, 9] = zero_rows[:2]
    px = px_ref[...]
    for pair in (3, 0, 1, 2):
        for g in range(2):
            rows = []
            for r in range(4 * g, 4 * g + 4):
                for s in range(4):
                    rows.append(
                        jnp.concatenate([x_ref[s, 2 * pair, r], x_ref[s, 2 * pair + 1, r]], axis=1)
                    )
            moved = mm(px, jnp.concatenate(rows, axis=0)).astype(BF)
            for f in range(2):
                xp[2 * pair + f, 1 + 4 * g : 5 + 4 * g] = moved[:, 128 * f : 128 * f + 128].reshape(4, 6, 16, 128)

    pl.semaphore_wait(barrier, DEV - 1 + 3)

    my_r, my_q = me // 4, me % 4
    spread(
        lambda peer: xp.at[pl.ds(6, 2), peer // 4 + 1, peer % 4 + 1],
        lambda mine: t1r.at[:, mine],
        0,
    )
    t1r[:, me] = xp[6:8, my_r + 1, my_q + 1]

    sa = sa_ref[...].astype(F32)
    opening = jnp.zeros((1, 128), jnp.bool_)
    first = jnp.int32(0)
    for n in range(16):
        opening = opening | (sa == first.astype(F32))
        first = first + cnt_ref[n]
    wanted = jnp.where(opening, -1000.0, sa * 4.0 - 4.0)
    codes = jnp.concatenate([sa * 4.0, wanted, jnp.zeros((14, 128), F32)], axis=0).astype(BF)
    wide = mm(codes, ex_ref[...])
    lane = lax.broadcasted_iota(jnp.int32, (1, 512), 1)
    kpat = ((lane >> 2) & 3).astype(F32)
    vrow = wide[0:1] + kpat
    wrow = wide[1:2] + kpat
    vcol = jnp.transpose(jnp.broadcast_to(vrow, (128, 512)))
    wcol = jnp.transpose(jnp.broadcast_to(wrow, (128, 512)))
    lane128 = lax.broadcasted_iota(jnp.int32, (1, 128), 1).astype(F32)
    for j in range(4):
        cols = slice(128 * j, 128 * j + 128)
        hot_t[:, cols] = jnp.where(wcol == vrow[:, cols], 1.0, 0.0).astype(BF)
        hot_u[:, cols] = jnp.where(vcol == lane128 * 4.0 + j, 1.0, 0.0).astype(BF)
        ids = lax.broadcasted_iota(jnp.int32, (128, 1), 0).astype(F32) * 4.0 + j
        hot_s[cols, :] = jnp.where(ids == vrow, 1.0, 0.0).astype(BF)

    def taps(t, tail):
        for kt in range(3):
            for kh in range(3):
                for kw in range(3):
                    tap = (kt * 3 + kh) * 3 + kw
                    if tail and kt < 2:
                        tile = xt[kt, kh : kh + 8, kw : kw + 4]
                    else:
                        tile = xp[2 * t - 2 + kt, kh : kh + 8, kw : kw + 4]
                    pat[pl.ds(512 * t, 512), 128 * tap : 128 * tap + 128] = tile.reshape(512, 128)

    def convolve(t):
        for half in range(2):
            rows = pat[pl.ds(512 * t + 256 * half, 256), :]
            cs[pl.ds(16 * half, 16), t] = mm(rows, w_ref[...]).astype(BF).reshape(16, 16, 256)

    def conv_frame(t, tail):
        taps(t, tail)
        convolve(t)
        spread(lambda peer: cs.at[peer, t], lambda mine: cr.at[mine, t], 2 + t)
        cr[me, t] = cs[me, t]

    def later(t, carry):
        conv_frame(t, False)
        return carry

    lax.fori_loop(1, 4, later, 0)

    landed(t1r.at[:, pl.ds(0, DEV - 1)], 0)
    both = jnp.concatenate([t1r[0].reshape(512, 128), t1r[1].reshape(512, 128)], axis=1)
    moved = mm(hot_t[...], both).astype(BF)
    t2s[0] = moved[:, :128].reshape(32, 16, 128)
    t2s[1] = moved[:, 128:].reshape(32, 16, 128)
    spread(lambda peer: t2s.at[:, peer], lambda mine: t2r.at[:, mine], 1)
    t2r[:, me] = t2s[:, me]

    pg = pg_ref[...]
    for t in range(4):
        for g in range(2):
            rows = []
            for r in range(4 * g, 4 * g + 4):
                for s in range(4):
                    rows.append(ug_ref[s, t, 16 * r : 16 * r + 16])
            moved = mm(pg, jnp.concatenate(rows, axis=0))
            at = (2 * t + g) * 256
            gt[:, at : at + 256] = jnp.transpose(moved).astype(BF)

    landed(t2r.at[:, pl.ds(0, DEV - 1)], 1)
    for f in range(2):
        tiles = t2r[f].reshape(8, 4, 16, 128)
        xt[f, 1:9, 1:5] = tiles
        up = mm(sh_ref[0:128], tiles[:, 0].reshape(128, 128)).astype(BF)
        down = mm(sh_ref[128:256], tiles[:, 3].reshape(128, 128)).astype(BF)
        xt[f, 1:9, 5] = up.reshape(8, 16, 128)
        xt[f, 1:9, 0] = down.reshape(8, 16, 128)
    conv_frame(0, True)

    def grad_block(n, carry):
        at = pl.multiple_of(n * 256, 256)
        part = mm(gt[...], pat[:, pl.ds(at, 256)])
        dw[pl.ds(at, 256), :] = jnp.transpose(part)
        return carry

    lax.fori_loop(0, 13, grad_block, 0)
    dw[3328:3456, :] = jnp.transpose(mm(gt[...], pat[:, 3328:3456]))
    dw[3456:3464, :] = jnp.zeros((8, 256), F32)

    def regroup(g, carry):
        block = dw[pl.ds(pl.multiple_of(216 * g, 8), 224), :]
        for j in range(8):
            gf[j // 4, j % 4, g] = block[27 * j : 27 * j + 32]
        return carry

    lax.fori_loop(0, 16, regroup, 0)
    for part in range(4):
        gbs[part] = gf[1 - core, part].astype(BF)
    partner = me + 1 - 2 * core

    def reduce_copy(source, target, index, where):
        return pltpu.make_async_remote_copy(
            src_ref=source, dst_ref=target, send_sem=red_send.at[index],
            recv_sem=red_recv.at[index], device_id=where, device_id_type=MESH,
        )

    core_copy = reduce_copy(gbs, r1, 12, {"ctx": partner})
    core_copy.start()

    def see(a, carry):
        row = lax.broadcasted_iota(jnp.int32, (128, 192), 0)
        col = lax.broadcasted_iota(jnp.int32, (128, 192), 1)
        span = 32 * a + (row & 31)
        when = span * 4 + (row >> 5)
        col_t = (col >= 48).astype(jnp.int32) + (col >= 96).astype(jnp.int32) + (col >= 144).astype(jnp.int32)
        other = 32 * a - 16 + col - 48 * col_t
        start = jnp.zeros((128, 192), jnp.int32)
        total = jnp.int32(0)
        for n in range(15):
            total = total + cnt_ref[n]
            start = jnp.where(span >= total, total, start)
        seen = (other >= start) & (other * 4 + col_t <= when)
        mask[a] = jnp.where(seen, 1.0, 0.0).astype(BF)
        return carry

    lax.fori_loop(0, 4, see, 0)
    ks[:, 0:16] = jnp.zeros((4, 16, 256), BF)
    vs[:, 0:16] = jnp.zeros((4, 16, 256), BF)

    for t in (1, 2, 3, 0):
        landed(cr.at[pl.ds(0, DEV - 1), t], 2 + t)
        sorted_rows = mm(hot_s[...], cr[:, t].reshape(512, 256)).astype(BF)
        for k in range(4):
            ys[k, t] = sorted_rows[128 * k : 128 * k + 128]

    lanes = lax.broadcasted_iota(jnp.int32, (1, 256), 1)
    heads = [(lanes >> 6) == h for h in range(4)]
    scale = jnp.zeros((1, 256), F32)
    for h in range(4):
        scale = jnp.where(heads[h], scale_ref[h] * LOG2E, scale)

    def cell(k):
        rows = jnp.concatenate([ys[k, t] for t in range(4)], axis=0)
        wide = rows.astype(F32)
        mean = jnp.mean(wide * wide, axis=1, keepdims=True)
        normed = (wide * lax.rsqrt(mean + 1e-6)).astype(BF)
        query = mm(normed, wqkv_ref[:, 0:256])
        sums = mm((query * query).astype(BF), hs_ref[...])
        query = (query * (lax.rsqrt(sums + 1e-6) * scale)).astype(BF)
        key = mm(normed, wqkv_ref[:, 256:512])
        sums = mm((key * key).astype(BF), hs_ref[...])
        key = (key * lax.rsqrt(sums + 1e-6)).astype(BF)
        value = mm(normed, wqkv_ref[:, 512:768]).astype(BF)
        for t in range(4):
            qs[t] = query[128 * t : 128 * t + 128]
            ks[t, 16:144] = key[128 * t : 128 * t + 128]
            vs[t, 16:144] = value[128 * t : 128 * t + 128]

        def tile(a, carry):
            at = pl.multiple_of(32 * a, 32)
            qa = jnp.concatenate([qs[t, pl.ds(at, 32)] for t in range(4)], axis=0)
            zero = jnp.zeros_like(qa)
            stacked = jnp.concatenate([jnp.where(heads[h], qa, zero) for h in range(4)], axis=0)
            keys = jnp.concatenate([ks[t, pl.ds(at, 48)] for t in range(4)], axis=0)
            vals = jnp.concatenate([vs[t, pl.ds(at, 48)] for t in range(4)], axis=0)
            scores = lax.dot_general(
                stacked, keys, (((1,), (1,)), ((), ())), preferred_element_type=F32
            )
            see_a = mask[a]
            weights = jnp.exp2(scores).astype(BF) * jnp.concatenate([see_a] * 4, axis=0)
            total = jnp.sum(weights.astype(F32), axis=1, keepdims=True)
            mixed = mm(weights, vals) / total
            joined = jnp.zeros((128, 256), F32)
            for h in range(4):
                joined = jnp.where(heads[h], mixed[128 * h : 128 * h + 128], joined)
            base = jnp.concatenate([ys[k, t, pl.ds(at, 32)] for t in range(4)], axis=0)
            done = (base.astype(F32) + mm(joined.astype(BF), wout_ref[...])).astype(BF)
            for t in range(4):
                osb[t, pl.ds(at, 32)] = done[32 * t : 32 * t + 32]
            return carry

        lax.fori_loop(0, 4, tile, 0)
        back = mm(hot_u[...], osb[...].reshape(512, 256)).astype(BF)
        rb[k] = back.reshape(32, 16, 256)
        spread(lambda peer: rb.at[k, peer], lambda mine: orv.at[mine, k], 6 + k)
        orv[me, k] = rb[k, me]

    cell(0)
    core_copy.wait()
    for part in range(4):
        s1b[part] = (gf[core, part] + r1[part].astype(F32)).astype(BF)
    acc1[...] = gf[core, z] + r1[z].astype(F32)
    z_copies = [
        reduce_copy(s1b.at[(z + d) % 4], r2.at[d - 1], d - 1, {"dp": (z + d) % 4}) for d in (1, 2, 3)
    ]
    for copy in z_copies:
        copy.start()
    cell(1)
    cell(2)
    for copy in z_copies:
        copy.wait()
    acc2[...] = acc1[...] + r2[0].astype(F32) + r2[1].astype(F32) + r2[2].astype(F32)
    s2b[...] = acc2[...].astype(BF)
    y_copies = []
    for d in (1, 2, 3):
        yp = (chip_y + d) % 4
        y_copies.append(
            reduce_copy(s2b.at[pl.ds(yp * 4, 4)], r3.at[d - 1], 2 + d, {"ctx": (yp * 4 + chip_x) * 2 + core})
        )
    for copy in y_copies:
        copy.start()
    cell(3)
    for copy in y_copies:
        copy.wait()
    acc3[...] = acc2[pl.ds(chip_y * 4, 4)] + r3[0].astype(F32) + r3[1].astype(F32) + r3[2].astype(F32)
    s3b[...] = acc3[...].astype(BF)
    x_copies = []
    for d in (1, 2, 3):
        xq = (chip_x + d) % 4
        x_copies.append(
            reduce_copy(s3b.at[xq], r4.at[d - 1], 5 + d, {"ctx": (chip_y * 4 + xq) * 2 + core})
        )
    for copy in x_copies:
        copy.start()
    for copy in x_copies:
        copy.wait()
    s4[...] = acc3[chip_x] + r4[0].astype(F32) + r4[1].astype(F32) + r4[2].astype(F32)
    end_copies = [
        reduce_copy(s4, r5.at[z], 8 + d, {"dp": (z + d) % 4}) for d in (1, 2, 3)
    ]
    for copy in end_copies:
        copy.start()
    r5[z] = s4[...]

    for k in range(4):
        landed(orv.at[pl.ds(0, DEV - 1), k], 6 + k)
    po = po_ref[...]
    for r in range(8):
        rows = orv[4 * r : 4 * r + 4].reshape(256, 256)
        moved = mm(po, rows).astype(BF)
        for s in range(4):
            for t in range(4):
                at = (s * 4 + t) * 16
                out_ref[s, t, 16 * r : 16 * r + 16] = moved[at : at + 16]
    for copy in end_copies:
        copy.wait()
    for part in range(4):
        cg_ref[27 * part : 27 * part + 27] = r5[part, 0:27]

    left(t1r.at[:, pl.ds(0, DEV - 1)], 0)
    left(t2s.at[:, pl.ds(0, DEV - 1)], 1)
    for t in range(4):
        left(cs.at[pl.ds(0, DEV - 1), t], 2 + t)
    for k in range(4):
        left(rb.at[k, pl.ds(0, DEV - 1)], 6 + k)


def per_device(pictures, slots, counts, scaling, taps, triple, final, upstream):
    vm = lambda shape, kind: pltpu.VMEM(shape, kind)
    scratch = [
        vm((8, 10, 6, 16, 128), BF),
        vm((2, 10, 6, 16, 128), BF),
        vm((2048, 3456), BF),
        vm((2, 32, 16, 128), BF),
        vm((2, 32, 16, 128), BF),
        vm((2, 32, 16, 128), BF),
        vm((32, 4, 16, 256), BF),
        vm((32, 4, 16, 256), BF),
        vm((256, 2048), BF),
        vm((3464, 256), F32),
        vm((2, 4, 16, 32, 256), F32),
        vm((4, 16, 32, 256), BF),
        vm((4, 16, 32, 256), BF),
        vm((4, 16, 32, 256), BF),
        vm((16, 32, 256), F32),
        vm((3, 16, 32, 256), BF),
        vm((16, 32, 256), BF),
        vm((16, 32, 256), F32),
        vm((3, 4, 32, 256), BF),
        vm((4, 32, 256), BF),
        vm((4, 32, 256), F32),
        vm((3, 32, 256), BF),
        vm((32, 256), F32),
        vm((4, 32, 256), F32),
        vm((512, 512), BF),
        vm((512, 512), BF),
        vm((512, 512), BF),
        vm((4, 128, 192), BF),
        vm((4, 4, 128, 256), BF),
        vm((4, 128, 256), BF),
        vm((4, 144, 256), BF),
        vm((4, 144, 256), BF),
        vm((4, 128, 256), BF),
        vm((4, 32, 16, 256), BF),
        vm((32, 4, 16, 256), BF),
        pltpu.SemaphoreType.DMA((10,)),
        pltpu.SemaphoreType.DMA((10,)),
        pltpu.SemaphoreType.DMA((13,)),
        pltpu.SemaphoreType.DMA((13,)),
    ]
    v = pl.BlockSpec(memory_space=pltpu.VMEM)
    s = pl.BlockSpec(memory_space=pltpu.SMEM)
    latents, conv_grad = pl.pallas_call(
        section_kernel,
        out_shape=(
            jax.ShapeDtypeStruct((4, 4, 128, 256), BF),
            jax.ShapeDtypeStruct((108, 256), F32),
        ),
        in_specs=[v, v, v, v, v, v, s, s, v, v, v, v, v, v],
        out_specs=(v, v),
        scratch_shapes=scratch,
        compiler_params=pltpu.CompilerParams(
            collective_id=0, has_side_effects=True, vmem_limit_bytes=62 * 1024 * 1024
        ),
    )(
        pictures[0], taps, triple, final, upstream[0], slots.reshape(1, 128), counts, scaling,
        frame_rows(), gradient_rows(), result_rows(), column_shifts(), slot_expand(), head_sums(),
    )
    return latents[None], conv_grad


def solution(mesh):
    placed = (
        P("dp", "ctx", None, None, None, None),
        P(), P(), P(), P(), P(), P(),
        P("dp", "ctx", None, None, None),
    )
    return jax.shard_map(
        per_device,
        mesh=mesh,
        in_specs=placed,
        out_specs=(P("dp", "ctx", None, None, None), P("ctx", None)),
        check_vma=False,
    )
```

time: 379 us -> 75.8 us (0.20)
  waiting for transfers between devices: 95.2 us -> 0 us
  blocking collectives: 83 us -> 0 us
  Pallas kernels: 0 us -> 70.8 us
  local copies, waits for them, and re-layouts: 67.8 us -> 2.97 us
  matrix products: 58.3 us -> 0 us
  other arithmetic: 42.9 us -> 0 us
  between operations: 15.1 us -> 0.65 us
  starting transfers between devices: 12.8 us -> 0 us
    unnamed x1 -> x0, blocking collectives: 83 us -> none
    pallas_call x0 -> x1, Pallas kernels: none -> 70.8 us  [per_device(): pl.pallas_call(section_kernel, out_shape=(jax.ShapeDtypeStruct((4, 4, 128...]
    dot_general x18 -> x0, matrix products: 58.3 us -> none  [the longest x4 18.9 us: timewise_softmax_mixing(): jnp.einsum('gahd,gbhd->ghab', queries, keys_all, precision=lax.Precision....]
    all_gather x1 -> x0, waiting for transfers between devices: 52.3 us -> none  [per_device(): shard_rows = lax.all_gather(tails, 'ctx', axis=0, tiled=True)]
    psum x1 -> x0, waiting for transfers between devices: 36.7 us -> none  [per_device(): conv_grad = lax.psum(grad_share, 'dp')]
    slice x17 -> x0, local copies, waits for them, and re-layouts: 25.5 us -> none  [the longest x4 8.24 us: timewise_softmax_mixing(): projected[..., channel_width:2 * channel_width].reshape(head_shape)]
    sub x5 -> x0, other arithmetic: 17.3 us -> none  [the longest x4 16.6 us: timewise_softmax_mixing(): weights = jnp.exp(affinity_logits - highest)]
    mul x8 -> x0, local copies, waits for them, and re-layouts: 16.4 us -> none  [the longest x4 8.22 us: timewise_softmax_mixing(): queries * queries]
  transfers between devices with their start and end apart: 6 -> 0, of which waited for: 3 -> 0; matrix products, arithmetic and copies ran while one was open for 27% -> 0% of each run, Pallas kernels for 0% -> 0%
where the time goes in v1:
time: 75.8 us; the launch traced here: 74.4 us
  Pallas kernels  70.8 us (93%)
  local copies, waits for them, and re-layouts  2.97 us (4%)
    pallas_call x1, Pallas kernels, per_device(): pl.pallas_call(section_kernel, out_shape=(jax.ShapeDtypeStruct((4, 4, 128...  70.8 us
    unnamed x4, local copies, waits for them, and re-layouts  2.97 us

profile of v1, /device:TPU:1, one launch (start us, length us, event | category | flops | bytes accessed | tf_op | source)
XLA Modules:
  0.0 74.4 jit_solution(10628025552194250182)
XLA Ops:
  0.6 70.8 %shard_map.149 = (bf16[4,4,128,256]{3,2,1,0:T(8,128)(2,1)}, f32[108,256]{1,0:T(8,128)}) custom-call(bf16[4,8,8,16,128]{4,3,2,1,0:T(8,128)(2,1)} %bitcast.5, bf16[3456,256]{1,0:T(8,128)(2,1)} %w_ref.1, bf16[256,768]{1,0:T(8,128)(2,1)} %wqkv_ref.1, bf16[256,256]{1,0:T(8,128)(2,1)} %wout_ref.1, bf16[4,4,128,256]{3,2,1,0:T(8,128)(2,1)} %bitcast.6, ...), custom_call_target="tpu_custom_call" | custom-call | tf_op jit(solution)/shard_map/pallas_call | solution.py:458
  71.5 0.0 copy-start
  71.5 2.3 %copy.18 = bf16[1,4,4,128,256]{4,3,2,1,0:T(8,128)(2,1)} copy(bf16[1,4,4,128,256]{4,3,2,1,0:T(8,128)(2,1)} %bitcast.4) | data formatting | bytes 2097152
  73.8 0.0 copy-done
  73.8 0.6 copy.19
Async XLA Ops:
  71.5 2.3 %copy-start = (f32[108,256]{1,0:T(8,128)S(1)}, f32[108,256]{1,0:T(8,128)}, u32[]{:S(2)}) copy-start(f32[108,256]{1,0:T(8,128)} %get-tuple-element.9) | copy-start | bytes 331780

commit v2 on v1

--- a/solution.py
+++ b/solution.py
@@ -83,33 +83,44 @@
 
 
 def section_kernel(
-    x_ref, w_ref, wqkv_ref, wout_ref, ug_ref, sa_ref, cnt_ref, scale_ref,
-    px_ref, pg_ref, po_ref, sh_ref, ex_ref, hs_ref,
+    x_hbm, w_hbm, wqkv_hbm, wout_hbm, ug_hbm, sa_ref, cnt_ref, scale_ref,
+    px_hbm, pg_hbm, po_hbm, sh_hbm, ex_hbm, hs_hbm,
     out_ref, cg_ref,
-    xp, xt, pat, t1r, t2s, t2r, cs, cr, gt, dw, gf, gbs, r1, s1b, acc1, r2, s2b, acc2, r3, s3b, acc3, r4, s4, r5,
+    x_ref, px_ref, ug_ref, pg_ref, w_ref, ex_ref, sh_ref, wqkv_ref, hs_ref, wout_ref, po_ref,
+    xp, xt, pat, t1r, t2s, t2r, cs, cr, gt, dwt, dw, gf, gbs, r1, s1b, zu, zd, acc2, s2b, r3, s3b, acc3, r4, s4, r5,
     hot_t, hot_s, hot_u, mask, ys, qs, ks, vs, osb, rb, orv,
-    send_sem, recv_sem, red_send, red_recv,
+    send_sem, recv_sem, red_send, red_recv, in_sem,
 ):
     z = lax.axis_index("dp")
     me = lax.axis_index("ctx")
-    core = me % 2
-    chip_x = (me // 2) % 4
-    chip_y = me // 8
+    core = me & 1
+    chip_x = (me >> 1) & 3
+    chip_y = me >> 3
+
+    loads = [
+        pltpu.make_async_copy(source, target, in_sem.at[n])
+        for n, (source, target) in enumerate((
+            (x_hbm, x_ref), (px_hbm, px_ref), (ug_hbm, ug_ref), (pg_hbm, pg_ref), (w_hbm, w_ref), (ex_hbm, ex_ref),
+            (sh_hbm, sh_ref), (wqkv_hbm, wqkv_ref), (hs_hbm, hs_ref), (wout_hbm, wout_ref), (po_hbm, po_ref),
+        ))
+    ]
+    for load in loads:
+        load.start()
 
     barrier = pltpu.get_barrier_semaphore()
 
     def greet(step, carry):
-        peer = (me + step) % DEV
+        peer = (me + step) & (DEV - 1)
         pl.semaphore_signal(barrier, inc=1, device_id={"ctx": peer}, device_id_type=MESH)
         return carry
 
     lax.fori_loop(1, DEV, greet, 0)
     for dz in range(1, 4):
-        pl.semaphore_signal(barrier, inc=1, device_id={"dp": (z + dz) % 4}, device_id_type=MESH)
+        pl.semaphore_signal(barrier, inc=1, device_id={"dp": (z + dz) & 3}, device_id_type=MESH)
 
     def spread(source, target, phase):
         def one(step, carry):
-            peer = (me + step) % DEV
+            peer = (me + step) & (DEV - 1)
             pltpu.make_async_remote_copy(
                 src_ref=source(peer), dst_ref=target(me), send_sem=send_sem.at[phase],
                 recv_sem=recv_sem.at[phase], device_id={"ctx": peer}, device_id_type=MESH,
@@ -129,6 +140,8 @@
     xp[:, 9] = zero_rows
     xt[:, 0] = zero_rows[:2]
     xt[:, 9] = zero_rows[:2]
+    loads[0].wait()
+    loads[1].wait()
     px = px_ref[...]
     for pair in (3, 0, 1, 2):
         for g in range(2):
@@ -142,16 +155,61 @@
             for f in range(2):
                 xp[2 * pair + f, 1 + 4 * g : 5 + 4 * g] = moved[:, 128 * f : 128 * f + 128].reshape(4, 6, 16, 128)
 
+    def taps(t, tail, kts):
+        for kt in kts:
+            for kh in range(3):
+                for kw in range(3):
+                    tap = (kt * 3 + kh) * 3 + kw
+                    if tail:
+                        tile = xt[kt, kh : kh + 8, kw : kw + 4]
+                    else:
+                        tile = xp[2 * t - 2 + kt, kh : kh + 8, kw : kw + 4]
+                    pat[pl.ds(512 * t, 512), 128 * tap : 128 * tap + 128] = tile.reshape(512, 128)
+
+    def convolve(t):
+        for half in range(2):
+            rows = pat[pl.ds(512 * t + 256 * half, 256), :]
+            cs[pl.ds(16 * half, 16), t] = mm(rows, w_ref[...]).astype(BF).reshape(16, 16, 256)
+        cr[me, t] = cs[me, t]
+
+    def send_frame(t):
+        spread(lambda peer: cs.at[peer, t], lambda mine: cr.at[mine, t], 2 + t)
+
+    loads[4].wait()
+    taps(1, False, (0, 1, 2))
+    convolve(1)
+    loads[2].wait()
+    loads[3].wait()
+    pg = pg_ref[...]
+    for t in range(4):
+        for g in range(2):
+            rows = []
+            for r in range(4 * g, 4 * g + 4):
+                for s in range(4):
+                    rows.append(ug_ref[s, t, 16 * r : 16 * r + 16])
+            moved = mm(pg, jnp.concatenate(rows, axis=0))
+            at = (2 * t + g) * 256
+            gt[:, at : at + 256] = jnp.transpose(moved).astype(BF)
     pl.semaphore_wait(barrier, DEV - 1 + 3)
 
-    my_r, my_q = me // 4, me % 4
+    my_r, my_q = me >> 2, me & 3
     spread(
-        lambda peer: xp.at[pl.ds(6, 2), peer // 4 + 1, peer % 4 + 1],
+        lambda peer: xp.at[pl.ds(6, 2), (peer >> 2) + 1, (peer & 3) + 1],
         lambda mine: t1r.at[:, mine],
         0,
     )
+    send_frame(1)
     t1r[:, me] = xp[6:8, my_r + 1, my_q + 1]
 
+    def later(t, carry):
+        taps(t, False, (0, 1, 2))
+        convolve(t)
+        return carry
+
+    lax.fori_loop(2, 4, later, 0)
+    taps(0, False, (2,))
+
+    loads[5].wait()
     sa = sa_ref[...].astype(F32)
     opening = jnp.zeros((1, 128), jnp.bool_)
     first = jnp.int32(0)
@@ -175,33 +233,14 @@
         ids = lax.broadcasted_iota(jnp.int32, (128, 1), 0).astype(F32) * 4.0 + j
         hot_s[cols, :] = jnp.where(ids == vrow, 1.0, 0.0).astype(BF)
 
-    def taps(t, tail):
-        for kt in range(3):
-            for kh in range(3):
-                for kw in range(3):
-                    tap = (kt * 3 + kh) * 3 + kw
-                    if tail and kt < 2:
-                        tile = xt[kt, kh : kh + 8, kw : kw + 4]
-                    else:
-                        tile = xp[2 * t - 2 + kt, kh : kh + 8, kw : kw + 4]
-                    pat[pl.ds(512 * t, 512), 128 * tap : 128 * tap + 128] = tile.reshape(512, 128)
-
-    def convolve(t):
-        for half in range(2):
-            rows = pat[pl.ds(512 * t + 256 * half, 256), :]
-            cs[pl.ds(16 * half, 16), t] = mm(rows, w_ref[...]).astype(BF).reshape(16, 16, 256)
-
-    def conv_frame(t, tail):
-        taps(t, tail)
-        convolve(t)
-        spread(lambda peer: cs.at[peer, t], lambda mine: cr.at[mine, t], 2 + t)
-        cr[me, t] = cs[me, t]
-
-    def later(t, carry):
-        conv_frame(t, False)
-        return carry
-
-    lax.fori_loop(1, 4, later, 0)
+    def grad_last(n, carry):
+        at = pl.multiple_of(2304 + n * 256, 256)
+        dw[pl.ds(at, 256), :] = jnp.transpose(mm(gt[...], pat[:, pl.ds(at, 256)]))
+        return carry
+
+    lax.fori_loop(0, 4, grad_last, 0)
+    dw[3328:3456, :] = jnp.transpose(mm(gt[...], pat[:, 3328:3456]))
+    dw[3456:3464, :] = jnp.zeros((8, 256), F32)
 
     landed(t1r.at[:, pl.ds(0, DEV - 1)], 0)
     both = jnp.concatenate([t1r[0].reshape(512, 128), t1r[1].reshape(512, 128)], axis=1)
@@ -210,19 +249,18 @@
     t2s[1] = moved[:, 128:].reshape(32, 16, 128)
     spread(lambda peer: t2s.at[:, peer], lambda mine: t2r.at[:, mine], 1)
     t2r[:, me] = t2s[:, me]
-
-    pg = pg_ref[...]
-    for t in range(4):
-        for g in range(2):
-            rows = []
-            for r in range(4 * g, 4 * g + 4):
-                for s in range(4):
-                    rows.append(ug_ref[s, t, 16 * r : 16 * r + 16])
-            moved = mm(pg, jnp.concatenate(rows, axis=0))
-            at = (2 * t + g) * 256
-            gt[:, at : at + 256] = jnp.transpose(moved).astype(BF)
+    send_frame(2)
+    send_frame(3)
+
+    def grad_main(n, carry):
+        at = pl.multiple_of(n * 256, 256)
+        dwt[:, pl.ds(at, 256)] = mm(gt[:, 512:2048], pat[512:2048, pl.ds(at, 256)])
+        return carry
+
+    lax.fori_loop(0, 9, grad_main, 0)
 
     landed(t2r.at[:, pl.ds(0, DEV - 1)], 1)
+    loads[6].wait()
     for f in range(2):
         tiles = t2r[f].reshape(8, 4, 16, 128)
         xt[f, 1:9, 1:5] = tiles
@@ -230,18 +268,17 @@
         down = mm(sh_ref[128:256], tiles[:, 3].reshape(128, 128)).astype(BF)
         xt[f, 1:9, 5] = up.reshape(8, 16, 128)
         xt[f, 1:9, 0] = down.reshape(8, 16, 128)
-    conv_frame(0, True)
-
-    def grad_block(n, carry):
+    taps(0, True, (0, 1))
+    convolve(0)
+    send_frame(0)
+
+    def grad_tail(n, carry):
         at = pl.multiple_of(n * 256, 256)
-        part = mm(gt[...], pat[:, pl.ds(at, 256)])
+        part = dwt[:, pl.ds(at, 256)] + mm(gt[:, 0:512], pat[0:512, pl.ds(at, 256)])
         dw[pl.ds(at, 256), :] = jnp.transpose(part)
         return carry
 
-    lax.fori_loop(0, 13, grad_block, 0)
-    dw[3328:3456, :] = jnp.transpose(mm(gt[...], pat[:, 3328:3456]))
-    dw[3456:3464, :] = jnp.zeros((8, 256), F32)
-
+    lax.fori_loop(0, 9, grad_tail, 0)
     def regroup(g, carry):
         block = dw[pl.ds(pl.multiple_of(216 * g, 8), 224), :]
         for j in range(8):
@@ -259,7 +296,7 @@
             recv_sem=red_recv.at[index], device_id=where, device_id_type=MESH,
         )
 
-    core_copy = reduce_copy(gbs, r1, 12, {"ctx": partner})
+    core_copy = reduce_copy(gbs, r1, 0, {"ctx": partner})
     core_copy.start()
 
     def see(a, carry):
@@ -288,6 +325,8 @@
         for k in range(4):
             ys[k, t] = sorted_rows[128 * k : 128 * k + 128]
 
+    for load in loads[7:10]:
+        load.wait()
     lanes = lax.broadcasted_iota(jnp.int32, (1, 256), 1)
     heads = [(lanes >> 6) == h for h in range(4)]
     scale = jnp.zeros((1, 256), F32)
@@ -340,48 +379,64 @@
         spread(lambda peer: rb.at[k, peer], lambda mine: orv.at[mine, k], 6 + k)
         orv[me, k] = rb[k, me]
 
-    cell(0)
+    above, below, across = (z + 1) & 3, (z + 3) & 3, (z + 2) & 3
     core_copy.wait()
     for part in range(4):
-        s1b[part] = (gf[core, part] + r1[part].astype(F32)).astype(BF)
-    acc1[...] = gf[core, z] + r1[z].astype(F32)
-    z_copies = [
-        reduce_copy(s1b.at[(z + d) % 4], r2.at[d - 1], d - 1, {"dp": (z + d) % 4}) for d in (1, 2, 3)
+        gf[core, part] = gf[core, part] + r1[part].astype(F32)
+        s1b[part] = gf[core, part].astype(BF)
+    low, high = pl.ds(0, 8), pl.ds(8, 8)
+    z_first = [
+        reduce_copy(s1b.at[across, low], zu.at[0], 1, {"dp": above}),
+        reduce_copy(s1b.at[across, high], zd.at[0], 2, {"dp": below}),
+        reduce_copy(s1b.at[above, high], zu.at[1], 3, {"dp": above}),
+        reduce_copy(s1b.at[below, low], zd.at[1], 4, {"dp": below}),
     ]
-    for copy in z_copies:
+    for copy in z_first:
+        copy.start()
+    cell(0)
+    z_first[0].wait()
+    z_first[1].wait()
+    s1b[above, 0:8] = (gf[core, above, 0:8] + zu[0].astype(F32)).astype(BF)
+    s1b[below, 8:16] = (gf[core, below, 8:16] + zd[0].astype(F32)).astype(BF)
+    z_second = [
+        reduce_copy(s1b.at[above, low], zu.at[2], 5, {"dp": above}),
+        reduce_copy(s1b.at[below, high], zd.at[2], 6, {"dp": below}),
+    ]
+    for copy in z_second:
         copy.start()
     cell(1)
-    cell(2)
-    for copy in z_copies:
+    for copy in z_first[2:] + z_second:
         copy.wait()
-    acc2[...] = acc1[...] + r2[0].astype(F32) + r2[1].astype(F32) + r2[2].astype(F32)
+    acc2[0:8] = gf[core, z, 0:8] + zu[2].astype(F32) + zd[1].astype(F32)
+    acc2[8:16] = gf[core, z, 8:16] + zu[1].astype(F32) + zd[2].astype(F32)
     s2b[...] = acc2[...].astype(BF)
     y_copies = []
     for d in (1, 2, 3):
-        yp = (chip_y + d) % 4
+        yp = (chip_y + d) & 3
         y_copies.append(
-            reduce_copy(s2b.at[pl.ds(yp * 4, 4)], r3.at[d - 1], 2 + d, {"ctx": (yp * 4 + chip_x) * 2 + core})
+            reduce_copy(s2b.at[pl.ds(yp * 4, 4)], r3.at[d - 1], 6 + d, {"ctx": (yp * 4 + chip_x) * 2 + core})
         )
     for copy in y_copies:
         copy.start()
-    cell(3)
+    cell(2)
     for copy in y_copies:
         copy.wait()
     acc3[...] = acc2[pl.ds(chip_y * 4, 4)] + r3[0].astype(F32) + r3[1].astype(F32) + r3[2].astype(F32)
     s3b[...] = acc3[...].astype(BF)
     x_copies = []
     for d in (1, 2, 3):
-        xq = (chip_x + d) % 4
+        xq = (chip_x + d) & 3
         x_copies.append(
-            reduce_copy(s3b.at[xq], r4.at[d - 1], 5 + d, {"ctx": (chip_y * 4 + xq) * 2 + core})
+            reduce_copy(s3b.at[xq], r4.at[d - 1], 9 + d, {"ctx": (chip_y * 4 + xq) * 2 + core})
         )
     for copy in x_copies:
         copy.start()
+    cell(3)
     for copy in x_copies:
         copy.wait()
     s4[...] = acc3[chip_x] + r4[0].astype(F32) + r4[1].astype(F32) + r4[2].astype(F32)
     end_copies = [
-        reduce_copy(s4, r5.at[z], 8 + d, {"dp": (z + d) % 4}) for d in (1, 2, 3)
+        reduce_copy(s4, r5.at[z], 12 + d, {"dp": (z + d) & 3}) for d in (1, 2, 3)
     ]
     for copy in end_copies:
         copy.start()
@@ -389,6 +444,7 @@
 
     for k in range(4):
         landed(orv.at[pl.ds(0, DEV - 1), k], 6 + k)
+    loads[10].wait()
     po = po_ref[...]
     for r in range(8):
         rows = orv[4 * r : 4 * r + 4].reshape(256, 256)
@@ -413,6 +469,17 @@
 def per_device(pictures, slots, counts, scaling, taps, triple, final, upstream):
     vm = lambda shape, kind: pltpu.VMEM(shape, kind)
     scratch = [
+        vm((4, 8, 8, 16, 128), BF),
+        vm((384, 256), BF),
+        vm((4, 4, 128, 256), BF),
+        vm((256, 256), BF),
+        vm((3456, 256), BF),
+        vm((128, 512), BF),
+        vm((256, 128), BF),
+        vm((256, 768), BF),
+        vm((256, 256), BF),
+        vm((256, 256), BF),
+        vm((256, 256), BF),
         vm((8, 10, 6, 16, 128), BF),
         vm((2, 10, 6, 16, 128), BF),
         vm((2048, 3456), BF),
@@ -422,15 +489,16 @@
         vm((32, 4, 16, 256), BF),
         vm((32, 4, 16, 256), BF),
         vm((256, 2048), BF),
+        vm((256, 2304), F32),
         vm((3464, 256), F32),
         vm((2, 4, 16, 32, 256), F32),
         vm((4, 16, 32, 256), BF),
         vm((4, 16, 32, 256), BF),
         vm((4, 16, 32, 256), BF),
+        vm((3, 8, 32, 256), BF),
+        vm((3, 8, 32, 256), BF),
         vm((16, 32, 256), F32),
-        vm((3, 16, 32, 256), BF),
         vm((16, 32, 256), BF),
-        vm((16, 32, 256), F32),
         vm((3, 4, 32, 256), BF),
         vm((4, 32, 256), BF),
         vm((4, 32, 256), F32),
@@ -450,18 +518,20 @@
         vm((32, 4, 16, 256), BF),
         pltpu.SemaphoreType.DMA((10,)),
         pltpu.SemaphoreType.DMA((10,)),
-        pltpu.SemaphoreType.DMA((13,)),
-        pltpu.SemaphoreType.DMA((13,)),
+        pltpu.SemaphoreType.DMA((16,)),
+        pltpu.SemaphoreType.DMA((16,)),
+        pltpu.SemaphoreType.DMA((11,)),
     ]
     v = pl.BlockSpec(memory_space=pltpu.VMEM)
     s = pl.BlockSpec(memory_space=pltpu.SMEM)
+    h = pl.BlockSpec(memory_space=pl.ANY)
     latents, conv_grad = pl.pallas_call(
         section_kernel,
         out_shape=(
             jax.ShapeDtypeStruct((4, 4, 128, 256), BF),
             jax.ShapeDtypeStruct((108, 256), F32),
         ),
-        in_specs=[v, v, v, v, v, v, s, s, v, v, v, v, v, v],
+        in_specs=[h, h, h, h, h, v, s, s, h, h, h, h, h, h],
         out_specs=(v, v),
         scratch_shapes=scratch,
         compiler_params=pltpu.CompilerParams(

time: 75.8 us -> 66.6 us (0.88); the launches traced: 74.4 us -> 66.5 us
  Pallas kernels: 70.8 us -> 62.9 us
    pallas_call x1, Pallas kernels: 70.8 us -> 62.9 us  [per_device(): pl.pallas_call(section_kernel, out_shape=(jax.ShapeDtypeStruct((4, 4, 128...]
where the time goes in v2:
time: 66.6 us; the launch traced here: 66.5 us
  Pallas kernels  62.9 us (94%)
  local copies, waits for them, and re-layouts  2.97 us (4%)
    pallas_call x1, Pallas kernels, per_device(): pl.pallas_call(section_kernel, out_shape=(jax.ShapeDtypeStruct((4, 4, 128...  62.9 us
    unnamed x4, local copies, waits for them, and re-layouts  2.97 us

profile of v2, /device:TPU:1, one launch (start us, length us, event | category | flops | bytes accessed | tf_op | source)
XLA Modules:
  0.0 66.5 jit_solution(3274676270629636647)
XLA Ops:
  0.6 62.9 %shard_map.149 = (bf16[4,4,128,256]{3,2,1,0:T(8,128)(2,1)}, f32[108,256]{1,0:T(8,128)}) custom-call(bf16[4,8,8,16,128]{4,3,2,1,0:T(8,128)(2,1)} %bitcast.5, bf16[3456,256]{1,0:T(8,128)(2,1)} %w_hbm.1, bf16[256,768]{1,0:T(8,128)(2,1)} %wqkv_hbm.1, bf16[256,256]{1,0:T(8,128)(2,1)} %wout_hbm.1, bf16[4,4,128,256]{3,2,1,0:T(8,128)(2,1)} %bitcast.6, ...), custom_call_target="tpu_custom_call" | custom-call | tf_op jit(solution)/shard_map/pallas_call | solution.py:528
  63.5 0.0 copy-start
  63.5 2.3 %copy.18 = bf16[1,4,4,128,256]{4,3,2,1,0:T(8,128)(2,1)} copy(bf16[1,4,4,128,256]{4,3,2,1,0:T(8,128)(2,1)} %bitcast.4) | data formatting | bytes 2097152
  65.8 0.0 copy-done
  65.8 0.6 copy.19
Async XLA Ops:
  63.5 2.3 %copy-start = (f32[108,256]{1,0:T(8,128)S(1)}, f32[108,256]{1,0:T(8,128)}, u32[]{:S(2)}) copy-start(f32[108,256]{1,0:T(8,128)} %get-tuple-element.9) | copy-start | bytes 331780

commit v3 on v2

v3 whole, which is shorter than its diff:
```python
import jax
import jax.numpy as jnp
import numpy as np
from jax import lax
from jax.experimental import pallas as pl
from jax.experimental.pallas import tpu as pltpu
from jax.sharding import PartitionSpec as P

BF = jnp.bfloat16
F32 = jnp.float32
MESH = pl.DeviceIdType.MESH
DEV = 32
UNROLL = 4
LOG2E = 1.4426950408889634


def one_hot_rows(rows, cols, pairs):
    table = np.zeros((rows, cols), np.float32)
    for row, col in pairs:
        table[row, col] = 1.0
    return jnp.asarray(table, BF)


def frame_rows():
    pairs = []
    for r in range(4):
        for qp in range(-1, 5):
            for k in range(4):
                for s in range(4):
                    q = qp + 4 * k
                    if 0 <= q < 16:
                        pairs.append((((r * 6 + qp + 1) * 4 + k) * 4 + s, (r * 4 + s) * 16 + q))
    return one_hot_rows(384, 256, pairs)


def gradient_rows():
    pairs = []
    for r in range(4):
        for qp in range(4):
            for k in range(4):
                for s in range(4):
                    pairs.append((((r * 4 + qp) * 4 + k) * 4 + s, (r * 4 + s) * 16 + qp + 4 * k))
    return one_hot_rows(256, 256, pairs)


def result_rows():
    pairs = []
    for qp in range(4):
        for k in range(4):
            for t in range(4):
                for s in range(4):
                    pairs.append(((s * 4 + t) * 16 + qp + 4 * k, ((qp * 4 + k) * 4 + t) * 4 + s))
    return one_hot_rows(256, 256, pairs)


def column_shifts():
    pairs = []
    for r in range(8):
        for k in range(4):
            for s in range(4):
                if k < 3:
                    pairs.append(((r * 4 + k) * 4 + s, (r * 4 + k + 1) * 4 + s))
                if k > 0:
                    pairs.append((128 + (r * 4 + k) * 4 + s, (r * 4 + k - 1) * 4 + s))
    return one_hot_rows(256, 128, pairs)


def slot_expand():
    pairs = []
    for e in range(32):
        for k in range(4):
            for s in range(4):
                pairs.append((4 * e + s, (e * 4 + k) * 4 + s))
    return one_hot_rows(128, 512, pairs)


def head_sums():
    table = np.kron(np.eye(4), np.ones((64, 64)))
    return jnp.asarray(table, BF)


def mm(a, b):
    return jnp.dot(a, b, preferred_element_type=F32)


def section_kernel(
    x_hbm, w_hbm, wqkv_hbm, wout_hbm, ug_hbm, sa_ref, cnt_ref, scale_ref,
    px_hbm, pg_hbm, sh_hbm, ex_hbm, hs_hbm,
    back_ref, rows_ref,
    x_ref, px_ref, ug_ref, pg_ref, w_ref, ex_ref, sh_ref, wqkv_ref, hs_ref, wout_ref,
    xp, xt, pat, t1r, t2s, t2r, cs, cr, gt, dwt, dw, gf, gbs, r1, s1b, r2, acc2, s2b, r3, s4,
    hot_t, hot_s, hot_u, mask, ys, qs, ks, vs, osb, rb,
    send_sem, recv_sem, red_send, red_recv, in_sem,
):
    z = lax.axis_index("dp")
    me = lax.axis_index("ctx")
    core = me & 1
    chip_x = (me >> 1) & 3
    chip_y = me >> 3

    loads = [
        pltpu.make_async_copy(source, target, in_sem.at[n])
        for n, (source, target) in enumerate((
            (x_hbm, x_ref), (px_hbm, px_ref), (ug_hbm, ug_ref), (pg_hbm, pg_ref), (w_hbm, w_ref), (ex_hbm, ex_ref),
            (sh_hbm, sh_ref), (wqkv_hbm, wqkv_ref), (hs_hbm, hs_ref), (wout_hbm, wout_ref),
        ))
    ]
    for load in loads:
        load.start()

    barrier = pltpu.get_barrier_semaphore()

    def greet(step, carry):
        peer = (me + step) & (DEV - 1)
        pl.semaphore_signal(barrier, inc=1, device_id={"ctx": peer}, device_id_type=MESH)
        return carry

    lax.fori_loop(1, DEV, greet, 0)
    for dz in range(1, 4):
        pl.semaphore_signal(barrier, inc=1, device_id={"dp": (z + dz) & 3}, device_id_type=MESH)

    def spread(source, target, phase):
        for step in range(1, DEV):
            peer = (me + step) & (DEV - 1)
            pltpu.make_async_remote_copy(
                src_ref=source(peer), dst_ref=target(me), send_sem=send_sem.at[phase],
                recv_sem=recv_sem.at[phase], device_id={"ctx": peer}, device_id_type=MESH,
            ).start()

    def landed(view, phase):
        pltpu.make_async_copy(view, view, recv_sem.at[phase]).wait()

    def left(view, phase):
        pltpu.make_async_copy(view, view, send_sem.at[phase]).wait()

    zero_rows = jnp.zeros((8, 6, 16, 128), BF)
    xp[:, 0] = zero_rows
    xp[:, 9] = zero_rows
    xt[:, 0] = zero_rows[:2]
    xt[:, 9] = zero_rows[:2]
    loads[0].wait()
    loads[1].wait()
    px = px_ref[...]
    for pair in (3, 0, 1, 2):
        for g in range(2):
            rows = []
            for r in range(4 * g, 4 * g + 4):
                for s in range(4):
                    rows.append(
                        jnp.concatenate([x_ref[s, 2 * pair, r], x_ref[s, 2 * pair + 1, r]], axis=1)
                    )
            moved = mm(px, jnp.concatenate(rows, axis=0)).astype(BF)
            for f in range(2):
                xp[2 * pair + f, 1 + 4 * g : 5 + 4 * g] = moved[:, 128 * f : 128 * f + 128].reshape(4, 6, 16, 128)

    def taps(t, tail, kts):
        for kt in kts:
            for kh in range(3):
                for kw in range(3):
                    tap = (kt * 3 + kh) * 3 + kw
                    if tail:
                        tile = xt[kt, kh : kh + 8, kw : kw + 4]
                    else:
                        tile = xp[2 * t - 2 + kt, kh : kh + 8, kw : kw + 4]
                    pat[pl.ds(512 * t, 512), 128 * tap : 128 * tap + 128] = tile.reshape(512, 128)

    def convolve(t):
        for half in range(2):
            rows = pat[pl.ds(512 * t + 256 * half, 256), :]
            cs[pl.ds(16 * half, 16), t] = mm(rows, w_ref[...]).astype(BF).reshape(16, 16, 256)
        cr[me, t] = cs[me, t]

    def send_frame(t):
        spread(lambda peer: cs.at[peer, t], lambda mine: cr.at[mine, t], 2 + t)

    loads[4].wait()
    taps(1, False, (0, 1, 2))
    convolve(1)
    loads[2].wait()
    loads[3].wait()
    pg = pg_ref[...]
    for t in range(4):
        for g in range(2):
            rows = []
            for r in range(4 * g, 4 * g + 4):
                for s in range(4):
                    rows.append(ug_ref[s, t, 16 * r : 16 * r + 16])
            moved = mm(pg, jnp.concatenate(rows, axis=0))
            at = (2 * t + g) * 256
            gt[:, at : at + 256] = jnp.transpose(moved).astype(BF)
    taps(2, False, (0, 1, 2))
    convolve(2)
    pl.semaphore_wait(barrier, DEV - 1 + 3)

    my_r, my_q = me >> 2, me & 3
    spread(
        lambda peer: xp.at[pl.ds(6, 2), (peer >> 2) + 1, (peer & 3) + 1],
        lambda mine: t1r.at[:, mine],
        0,
    )
    send_frame(1)
    t1r[:, me] = xp[6:8, my_r + 1, my_q + 1]

    taps(3, False, (0, 1, 2))
    convolve(3)
    taps(0, False, (2,))

    loads[5].wait()
    sa = sa_ref[...].astype(F32)
    opening = jnp.zeros((1, 128), jnp.bool_)
    first = jnp.int32(0)
    for n in range(16):
        opening = opening | (sa == first.astype(F32))
        first = first + cnt_ref[n]
    wanted = jnp.where(opening, -1000.0, sa * 4.0 - 4.0)
    codes = jnp.concatenate([sa * 4.0, wanted, jnp.zeros((14, 128), F32)], axis=0).astype(BF)
    wide = mm(codes, ex_ref[...])
    lane = lax.broadcasted_iota(jnp.int32, (1, 512), 1)
    kpat = ((lane >> 2) & 3).astype(F32)
    vrow = wide[0:1] + kpat
    wrow = wide[1:2] + kpat
    vcol = jnp.transpose(jnp.broadcast_to(vrow, (128, 512)))
    wcol = jnp.transpose(jnp.broadcast_to(wrow, (128, 512)))
    lane128 = lax.broadcasted_iota(jnp.int32, (1, 128), 1).astype(F32)
    for j in range(4):
        cols = slice(128 * j, 128 * j + 128)
        hot_t[:, cols] = jnp.where(wcol == vrow[:, cols], 1.0, 0.0).astype(BF)
        hot_u[:, cols] = jnp.where(vcol == lane128 * 4.0 + j, 1.0, 0.0).astype(BF)
        ids = lax.broadcasted_iota(jnp.int32, (128, 1), 0).astype(F32) * 4.0 + j
        hot_s[cols, :] = jnp.where(ids == vrow, 1.0, 0.0).astype(BF)

    def see(a, carry):
        row = lax.broadcasted_iota(jnp.int32, (128, 192), 0)
        col = lax.broadcasted_iota(jnp.int32, (128, 192), 1)
        span = 32 * a + (row & 31)
        when = span * 4 + (row >> 5)
        col_t = (col >= 48).astype(jnp.int32) + (col >= 96).astype(jnp.int32) + (col >= 144).astype(jnp.int32)
        other = 32 * a - 16 + col - 48 * col_t
        start = jnp.zeros((128, 192), jnp.int32)
        total = jnp.int32(0)
        for n in range(15):
            total = total + cnt_ref[n]
            start = jnp.where(span >= total, total, start)
        seen = (other >= start) & (other * 4 + col_t <= when)
        mask[a] = jnp.where(seen, 1.0, 0.0).astype(BF)
        return carry

    lax.fori_loop(0, 4, see, 0)
    ks[:, :, 0:16] = jnp.zeros((4, 4, 16, 256), BF)
    vs[:, :, :, 0:16, 0:128] = jnp.zeros((2, 4, 4, 16, 128), BF)
    vs[:, :, :, :, 128:256] = jnp.ones((2, 4, 4, 144, 128), BF)


    def grad_last(n, carry):
        at = pl.multiple_of(2304 + n * 256, 256)
        dw[pl.ds(at, 256), :] = jnp.transpose(mm(gt[...], pat[:, pl.ds(at, 256)]))
        return carry

    lax.fori_loop(0, 4, grad_last, 0)
    dw[3328:3456, :] = jnp.transpose(mm(gt[...], pat[:, 3328:3456]))
    dw[3456:3464, :] = jnp.zeros((8, 256), F32)

    partner = me + 1 - 2 * core

    def reduce_copy(source, target, index, where):
        return pltpu.make_async_remote_copy(
            src_ref=source, dst_ref=target, send_sem=red_send.at[index],
            recv_sem=red_recv.at[index], device_id=where, device_id_type=MESH,
        )

    def regroup(g, carry):
        block = dw[pl.ds(pl.multiple_of(216 * g, 8), 224), :]
        for j in range(8):
            gf[j // 4, j % 4, g] = block[27 * j : 27 * j + 32]
        return carry

    def to_partner(first, last, index):
        lax.fori_loop(first, last, regroup, 0)
        for part in range(4):
            gbs[part, first:last] = gf[1 - core, part, first:last].astype(BF)
        span = pl.ds(first, last - first)
        copies = [
            reduce_copy(gbs.at[part, span], r1.at[part, span], index, {"ctx": partner}) for part in range(4)
        ]
        for copy in copies:
            copy.start()

    def to_planes(first, last, index):
        span = pl.ds(first, last - first)
        pltpu.make_async_copy(r1.at[:, span], r1.at[:, span], red_recv.at[index]).wait()
        for part in range(4):
            whole = gf[core, part, first:last] + r1[part, first:last].astype(F32)
            gf[core, part, first:last] = whole
            s1b[part, first:last] = whole.astype(BF)
        copies = [
            reduce_copy(s1b.at[(z + d) & 3, span], r2.at[d - 1, span], index + d, {"dp": (z + d) & 3}) for d in (1, 3, 2)
        ]
        for copy in copies:
            copy.start()
        return copies

    to_partner(11, 16, 0)

    landed(t1r.at[:, pl.ds(0, DEV - 1)], 0)
    both = jnp.concatenate([t1r[0].reshape(512, 128), t1r[1].reshape(512, 128)], axis=1)
    moved = mm(hot_t[...], both).astype(BF)
    t2s[0] = moved[:, :128].reshape(32, 16, 128)
    t2s[1] = moved[:, 128:].reshape(32, 16, 128)
    spread(lambda peer: t2s.at[:, peer], lambda mine: t2r.at[:, mine], 1)
    t2r[:, me] = t2s[:, me]

    def grad_main(n, carry):
        at = pl.multiple_of(n * 256, 256)
        dwt[:, pl.ds(at, 256)] = mm(gt[:, 512:2048], pat[512:2048, pl.ds(at, 256)])
        return carry

    lax.fori_loop(0, 3, grad_main, 0)
    send_frame(2)
    send_frame(3)
    lax.fori_loop(3, 9, grad_main, 0)

    for load in loads[7:10]:
        load.wait()
    lanes = lax.broadcasted_iota(jnp.int32, (1, 256), 1)
    heads = [(lanes >> 6) == h for h in range(4)]
    left_half = lax.broadcasted_iota(jnp.int32, (1, 128), 1) < 64
    scale = jnp.zeros((1, 256), F32)
    for h in range(4):
        scale = jnp.where(heads[h], scale_ref[h] * LOG2E, scale)

    def stream_rows(t):
        landed(cr.at[pl.ds(0, DEV - 1), t], 2 + t)
        rows = mm(hot_s[...], cr[:, t].reshape(512, 256)).astype(BF)
        wide = rows.astype(F32)
        mean = jnp.mean(wide * wide, axis=1, keepdims=True)
        normed = (wide * lax.rsqrt(mean + 1e-6)).astype(BF)
        query = mm(normed, wqkv_ref[:, 0:256])
        sums = mm((query * query).astype(BF), hs_ref[...])
        query = (query * (lax.rsqrt(sums + 1e-6) * scale)).astype(BF)
        key = mm(normed, wqkv_ref[:, 256:512])
        sums = mm((key * key).astype(BF), hs_ref[...])
        key = (key * lax.rsqrt(sums + 1e-6)).astype(BF)
        value = mm(normed, wqkv_ref[:, 512:768]).astype(BF)
        for k in range(4):
            mine = slice(128 * k, 128 * k + 128)
            ys[k, t] = rows[mine]
            qs[k, t] = query[mine]
            ks[k, t, 16:144] = key[mine]
            for p in range(2):
                vs[p, k, t, 16:144, 0:128] = value[mine, 128 * p : 128 * p + 128]

    stream_rows(1)
    z_copies = to_planes(11, 16, 0)
    landed(t2r.at[:, pl.ds(0, DEV - 1)], 1)
    loads[6].wait()
    for f in range(2):
        tiles = t2r[f].reshape(8, 4, 16, 128)
        xt[f, 1:9, 1:5] = tiles
        up = mm(sh_ref[0:128], tiles[:, 0].reshape(128, 128)).astype(BF)
        down = mm(sh_ref[128:256], tiles[:, 3].reshape(128, 128)).astype(BF)
        xt[f, 1:9, 5] = up.reshape(8, 16, 128)
        xt[f, 1:9, 0] = down.reshape(8, 16, 128)
    taps(0, True, (0, 1))
    convolve(0)
    send_frame(0)

    def grad_tail(n, carry):
        at = pl.multiple_of(n * 256, 256)
        part = dwt[:, pl.ds(at, 256)] + mm(gt[:, 0:512], pat[0:512, pl.ds(at, 256)])
        dw[pl.ds(at, 256), :] = jnp.transpose(part)
        return carry

    lax.fori_loop(0, 9, grad_tail, 0, unroll=3)
    to_partner(0, 11, 4)


    stream_rows(2)
    stream_rows(3)
    def cell(k):
        def tile(a, carry):
            at = pl.multiple_of(32 * a, 32)
            see_a = jnp.concatenate([mask[a]] * 2, axis=0)
            joined = []
            for p in range(2):
                pair = slice(128 * p, 128 * p + 128)
                qa = jnp.concatenate([qs[k, t, pl.ds(at, 32), pair] for t in range(4)], axis=0)
                zero = jnp.zeros_like(qa)
                stacked = jnp.concatenate([jnp.where(left_half, qa, zero), jnp.where(left_half, zero, qa)], axis=0)
                keys = jnp.concatenate([ks[k, t, pl.ds(at, 48), pair] for t in range(4)], axis=0)
                vals = jnp.concatenate([vs[p, k, t, pl.ds(at, 48)] for t in range(4)], axis=0)
                scores = lax.dot_general(
                    stacked, keys, (((1,), (1,)), ((), ())), preferred_element_type=F32
                )
                weights = jnp.exp2(scores).astype(BF) * see_a
                both = mm(weights, vals)
                above_line = jnp.where(left_half, both[0:128, 0:128], both[128:256, 0:128])
                below_line = jnp.where(left_half, both[0:128, 128:256], both[128:256, 128:256])
                joined.append((above_line / below_line).astype(BF))
            joined = jnp.concatenate(joined, axis=1)
            base = jnp.concatenate([ys[k, t, pl.ds(at, 32)] for t in range(4)], axis=0)
            done = (base.astype(F32) + mm(joined, wout_ref[...])).astype(BF)
            for t in range(4):
                osb[t, pl.ds(at, 32)] = done[32 * t : 32 * t + 32]
            return carry

        lax.fori_loop(0, 4, tile, 0, unroll=UNROLL)

    def ship(k):
        back = mm(hot_u[...], osb[...].reshape(512, 256)).astype(BF)
        rb[k] = back.reshape(32, 16, 256)
        spread(lambda peer: rb.at[k, peer], lambda mine: back_ref.at[mine, k], 6 + k)
        back_ref[me, k] = rb[k, me]

    z_copies += to_planes(0, 11, 4)
    stream_rows(0)
    for k in range(3):
        cell(k)
        ship(k)
    cell(3)

    for copy in z_copies:
        copy.wait()
    acc2[...] = gf[core, z] + r2[0].astype(F32) + r2[1].astype(F32) + r2[2].astype(F32)
    s2b[...] = acc2[...].astype(BF)
    chip = me >> 1
    plane_copies = []
    for d in range(1, 16):
        other = (chip + d) & 15
        plane_copies.append(reduce_copy(s2b.at[other], r3.at[d - 1], 8, {"ctx": other * 2 + core}))
    for copy in plane_copies:
        copy.start()
    ship(3)

    pltpu.make_async_copy(r3, r3, red_recv.at[8]).wait()
    total = acc2[chip]
    for d in range(15):
        total = total + r3[d].astype(F32)
    s4[...] = total
    end_copies = [
        reduce_copy(s4, rows_ref.at[z], 8 + d, {"dp": (z + d) & 3}) for d in (1, 2, 3)
    ]
    for copy in end_copies:
        copy.start()
    rows_ref[z] = s4[...]
    for k in range(4):
        landed(back_ref.at[pl.ds(0, DEV - 1), k], 6 + k)
    left(t1r.at[:, pl.ds(0, DEV - 1)], 0)
    left(t2s.at[:, pl.ds(0, DEV - 1)], 1)
    for t in range(4):
        left(cs.at[pl.ds(0, DEV - 1), t], 2 + t)
    for k in range(4):
        left(rb.at[k, pl.ds(0, DEV - 1)], 6 + k)
    pltpu.make_async_copy(r3, r3, red_send.at[8]).wait()
    for span, index in ((pl.ds(11, 5), 0), (pl.ds(0, 11), 4)):
        pltpu.make_async_copy(gbs.at[:, span], gbs.at[:, span], red_send.at[index]).wait()
    for copy in end_copies:
        copy.wait()


def place_kernel(back_ref, rows_ref, po_ref, out_ref, cg_ref):
    for r in range(8):
        moved = mm(po_ref[...], back_ref[4 * r : 4 * r + 4].reshape(256, 256)).astype(BF)
        for s in range(4):
            for t in range(4):
                at = (s * 4 + t) * 16
                out_ref[s, t, 16 * r : 16 * r + 16] = moved[at : at + 16]
    for part in range(4):
        cg_ref[27 * part : 27 * part + 27] = rows_ref[part, 0:27]


def per_device(pictures, slots, counts, scaling, taps, triple, final, upstream):
    vm = lambda shape, kind: pltpu.VMEM(shape, kind)
    scratch = [
        vm((4, 8, 8, 16, 128), BF),
        vm((384, 256), BF),
        vm((4, 4, 128, 256), BF),
        vm((256, 256), BF),
        vm((3456, 256), BF),
        vm((128, 512), BF),
        vm((256, 128), BF),
        vm((256, 768), BF),
        vm((256, 256), BF),
        vm((256, 256), BF),
        vm((8, 10, 6, 16, 128), BF),
        vm((2, 10, 6, 16, 128), BF),
        vm((2048, 3456), BF),
        vm((2, 32, 16, 128), BF),
        vm((2, 32, 16, 128), BF),
        vm((2, 32, 16, 128), BF),
        vm((32, 4, 16, 256), BF),
        vm((32, 4, 16, 256), BF),
        vm((256, 2048), BF),
        vm((256, 2304), F32),
        vm((3464, 256), F32),
        vm((2, 4, 16, 32, 256), F32),
        vm((4, 16, 32, 256), BF),
        vm((4, 16, 32, 256), BF),
        vm((4, 16, 32, 256), BF),
        vm((3, 16, 32, 256), BF),
        vm((16, 32, 256), F32),
        vm((16, 32, 256), BF),
        vm((15, 32, 256), BF),
        vm((32, 256), F32),
        vm((512, 512), BF),
        vm((512, 512), BF),
        vm((512, 512), BF),
        vm((4, 128, 192), BF),
        vm((4, 4, 128, 256), BF),
        vm((4, 4, 128, 256), BF),
        vm((4, 4, 144, 256), BF),
        vm((2, 4, 4, 144, 256), BF),
        vm((4, 128, 256), BF),
        vm((4, 32, 16, 256), BF),
        pltpu.SemaphoreType.DMA((10,)),
        pltpu.SemaphoreType.DMA((10,)),
        pltpu.SemaphoreType.DMA((12,)),
        pltpu.SemaphoreType.DMA((12,)),
        pltpu.SemaphoreType.DMA((10,)),
    ]
    v = pl.BlockSpec(memory_space=pltpu.VMEM)
    s = pl.BlockSpec(memory_space=pltpu.SMEM)
    h = pl.BlockSpec(memory_space=pl.ANY)
    back, rows = pl.pallas_call(
        section_kernel,
        out_shape=(
            jax.ShapeDtypeStruct((32, 4, 16, 256), BF),
            jax.ShapeDtypeStruct((4, 32, 256), F32),
        ),
        in_specs=[h, h, h, h, h, v, s, s, h, h, h, h, h],
        out_specs=(v, v),
        scratch_shapes=scratch,
        compiler_params=pltpu.CompilerParams(
            collective_id=0, has_side_effects=True, vmem_limit_bytes=62 * 1024 * 1024
        ),
    )(
        pictures[0], taps, triple, final, upstream[0], slots.reshape(1, 128), counts, scaling,
        frame_rows(), gradient_rows(), column_shifts(), slot_expand(), head_sums(),
    )
    latents, conv_grad = pl.pallas_call(
        place_kernel,
        out_shape=(
            jax.ShapeDtypeStruct((4, 4, 128, 256), BF),
            jax.ShapeDtypeStruct((108, 256), F32),
        ),
        in_specs=[v, v, v],
        out_specs=(v, v),
    )(back, rows, result_rows())
    return latents[None], conv_grad


def solution(mesh):
    placed = (
        P("dp", "ctx", None, None, None, None),
        P(), P(), P(), P(), P(), P(),
        P("dp", "ctx", None, None, None),
    )
    return jax.shard_map(
        per_device,
        mesh=mesh,
        in_specs=placed,
        out_specs=(P("dp", "ctx", None, None, None), P("ctx", None)),
        check_vma=False,
    )
```

time: 66.6 us -> 57.8 us (0.87); the launches traced: 66.5 us -> 56.7 us
  Pallas kernels: 62.9 us -> 56.1 us
  local copies, waits for them, and re-layouts: 2.97 us -> 0 us
    pallas_call x1 -> x2, Pallas kernels: 62.9 us -> 56.1 us  [the longest x1 53.4 us: per_device(): pl.pallas_call(section_kernel, out_shape=(jax.ShapeDtypeStruct((32, 4, 16...]
    unnamed x4 -> x0, local copies, waits for them, and re-layouts: 2.97 us -> none
where the time goes in v3:
time: 57.8 us; the launch traced here: 56.7 us
  Pallas kernels  56.1 us (97%)
  between operations  0.64 us (1%)
    pallas_call x1, Pallas kernels, per_device(): pl.pallas_call(section_kernel, out_shape=(jax.ShapeDtypeStruct((32, 4, 16...  53.4 us
    pallas_call x1, Pallas kernels, per_device(): pl.pallas_call(place_kernel, out_shape=(jax.ShapeDtypeStruct((4, 4, 128,...  2.72 us

profile of v3, /device:TPU:1, one launch (start us, length us, event | category | flops | bytes accessed | tf_op | source)
XLA Modules:
  0.0 56.7 jit_solution(12893335342656510848)
XLA Ops:
  0.6 53.4 %shard_map.149 = (bf16[32,4,16,256]{3,2,1,0:T(8,128)(2,1)}, f32[4,32,256]{2,1,0:T(8,128)}) custom-call(bf16[4,8,8,16,128]{4,3,2,1,0:T(8,128)(2,1)} %bitcast.4, bf16[3456,256]{1,0:T(8,128)(2,1)} %w_hbm.1, bf16[256,768]{1,0:T(8,128)(2,1)} %wqkv_hbm.1, bf16[256,256]{1,0:T(8,128)(2,1)} %wout_hbm.1, bf16[4,4,128,256]{3,2,1,0:T(8,128)(2,1)} %bitcast.5, ...), custom_call_target="tpu_custom_call" | custom-call | tf_op jit(solution)/shard_map/pallas_call | solution.py:523
  54.0 2.7 %shard_map.150 = (bf16[4,4,128,256]{3,2,1,0:T(8,128)(2,1)}, f32[108,256]{1,0:T(8,128)}) custom-call(bf16[32,4,16,256]{3,2,1,0:T(8,128)(2,1)} %get-tuple-element.6.back_ref, f32[4,32,256]{2,1,0:T(8,128)} %get-tuple-element.7.rows_ref, bf16[256,256]{1,0:T(8,128)(2,1)} %constant.17.clone.po_ref), custom_call_target="tpu_custom_call" | custom-call | tf_op jit(solution)/shard_map/pallas_call | solution.py:539

commit v4 on v3

--- a/solution.py
+++ b/solution.py
@@ -105,19 +105,18 @@
             (sh_hbm, sh_ref), (wqkv_hbm, wqkv_ref), (hs_hbm, hs_ref), (wout_hbm, wout_ref),
         ))
     ]
-    for load in loads:
+    for load in loads[:2]:
         load.start()
 
     barrier = pltpu.get_barrier_semaphore()
 
-    def greet(step, carry):
+    for step in range(1, DEV):
         peer = (me + step) & (DEV - 1)
         pl.semaphore_signal(barrier, inc=1, device_id={"ctx": peer}, device_id_type=MESH)
-        return carry
-
-    lax.fori_loop(1, DEV, greet, 0)
     for dz in range(1, 4):
         pl.semaphore_signal(barrier, inc=1, device_id={"dp": (z + dz) & 3}, device_id_type=MESH)
+    for load in loads[2:]:
+        load.start()
 
     def spread(source, target, phase):
         for step in range(1, DEV):
@@ -141,7 +140,7 @@
     loads[0].wait()
     loads[1].wait()
     px = px_ref[...]
-    for pair in (3, 0, 1, 2):
+    def frames_in(pair):
         for g in range(2):
             rows = []
             for r in range(4 * g, 4 * g + 4):
@@ -153,6 +152,56 @@
             for f in range(2):
                 xp[2 * pair + f, 1 + 4 * g : 5 + 4 * g] = moved[:, 128 * f : 128 * f + 128].reshape(4, 6, 16, 128)
 
+    frames_in(3)
+    pl.semaphore_wait(barrier, DEV - 1 + 3)
+    my_r, my_q = me >> 2, me & 3
+    spread(
+        lambda peer: xp.at[pl.ds(6, 2), (peer >> 2) + 1, (peer & 3) + 1],
+        lambda mine: t1r.at[:, mine],
+        0,
+    )
+    t1r[:, me] = xp[6:8, my_r + 1, my_q + 1]
+    for pair in (0, 1, 2):
+        frames_in(pair)
+    partner = me + 1 - 2 * core
+
+    def reduce_copy(source, target, index, where):
+        return pltpu.make_async_remote_copy(
+            src_ref=source, dst_ref=target, send_sem=red_send.at[index],
+            recv_sem=red_recv.at[index], device_id=where, device_id_type=MESH,
+        )
+
+    def regroup(g, carry):
+        block = dw[pl.ds(pl.multiple_of(216 * g, 8), 224), :]
+        for j in range(8):
+            gf[j // 4, j % 4, g] = block[27 * j : 27 * j + 32]
+        return carry
+
+    def to_partner(first, last, index):
+        lax.fori_loop(first, last, regroup, 0)
+        for part in range(4):
+            gbs[part, first:last] = gf[1 - core, part, first:last].astype(BF)
+        span = pl.ds(first, last - first)
+        copies = [
+            reduce_copy(gbs.at[part, span], r1.at[part, span], index, {"ctx": partner}) for part in range(4)
+        ]
+        for copy in copies:
+            copy.start()
+
+    def to_planes(first, last, index):
+        span = pl.ds(first, last - first)
+        pltpu.make_async_copy(r1.at[:, span], r1.at[:, span], red_recv.at[index]).wait()
+        for part in range(4):
+            whole = gf[core, part, first:last] + r1[part, first:last].astype(F32)
+            gf[core, part, first:last] = whole
+            s1b[part, first:last] = whole.astype(BF)
+        copies = [
+            reduce_copy(s1b.at[(z + d) & 3, span], r2.at[d - 1, span], index + d, {"dp": (z + d) & 3}) for d in (1, 3, 2)
+        ]
+        for copy in copies:
+            copy.start()
+        return copies
+
     def taps(t, tail, kts):
         for kt in kts:
             for kh in range(3):
@@ -176,6 +225,7 @@
     loads[4].wait()
     taps(1, False, (0, 1, 2))
     convolve(1)
+    send_frame(1)
     loads[2].wait()
     loads[3].wait()
     pg = pg_ref[...]
@@ -190,17 +240,6 @@
             gt[:, at : at + 256] = jnp.transpose(moved).astype(BF)
     taps(2, False, (0, 1, 2))
     convolve(2)
-    pl.semaphore_wait(barrier, DEV - 1 + 3)
-
-    my_r, my_q = me >> 2, me & 3
-    spread(
-        lambda peer: xp.at[pl.ds(6, 2), (peer >> 2) + 1, (peer & 3) + 1],
-        lambda mine: t1r.at[:, mine],
-        0,
-    )
-    send_frame(1)
-    t1r[:, me] = xp[6:8, my_r + 1, my_q + 1]
-
     taps(3, False, (0, 1, 2))
     convolve(3)
     taps(0, False, (2,))
@@ -251,56 +290,6 @@
     vs[:, :, :, :, 128:256] = jnp.ones((2, 4, 4, 144, 128), BF)
 
 
-    def grad_last(n, carry):
-        at = pl.multiple_of(2304 + n * 256, 256)
-        dw[pl.ds(at, 256), :] = jnp.transpose(mm(gt[...], pat[:, pl.ds(at, 256)]))
-        return carry
-
-    lax.fori_loop(0, 4, grad_last, 0)
-    dw[3328:3456, :] = jnp.transpose(mm(gt[...], pat[:, 3328:3456]))
-    dw[3456:3464, :] = jnp.zeros((8, 256), F32)
-
-    partner = me + 1 - 2 * core
-
-    def reduce_copy(source, target, index, where):
-        return pltpu.make_async_remote_copy(
-            src_ref=source, dst_ref=target, send_sem=red_send.at[index],
-            recv_sem=red_recv.at[index], device_id=where, device_id_type=MESH,
-        )
-
-    def regroup(g, carry):
-        block = dw[pl.ds(pl.multiple_of(216 * g, 8), 224), :]
-        for j in range(8):
-            gf[j // 4, j % 4, g] = block[27 * j : 27 * j + 32]
-        return carry
-
-    def to_partner(first, last, index):
-        lax.fori_loop(first, last, regroup, 0)
-        for part in range(4):
-            gbs[part, first:last] = gf[1 - core, part, first:last].astype(BF)
-        span = pl.ds(first, last - first)
-        copies = [
-            reduce_copy(gbs.at[part, span], r1.at[part, span], index, {"ctx": partner}) for part in range(4)
-        ]
-        for copy in copies:
-            copy.start()
-
-    def to_planes(first, last, index):
-        span = pl.ds(first, last - first)
-        pltpu.make_async_copy(r1.at[:, span], r1.at[:, span], red_recv.at[index]).wait()
-        for part in range(4):
-            whole = gf[core, part, first:last] + r1[part, first:last].astype(F32)
-            gf[core, part, first:last] = whole
-            s1b[part, first:last] = whole.astype(BF)
-        copies = [
-            reduce_copy(s1b.at[(z + d) & 3, span], r2.at[d - 1, span], index + d, {"dp": (z + d) & 3}) for d in (1, 3, 2)
-        ]
-        for copy in copies:
-            copy.start()
-        return copies
-
-    to_partner(11, 16, 0)
-
     landed(t1r.at[:, pl.ds(0, DEV - 1)], 0)
     both = jnp.concatenate([t1r[0].reshape(512, 128), t1r[1].reshape(512, 128)], axis=1)
     moved = mm(hot_t[...], both).astype(BF)
@@ -308,6 +297,18 @@
     t2s[1] = moved[:, 128:].reshape(32, 16, 128)
     spread(lambda peer: t2s.at[:, peer], lambda mine: t2r.at[:, mine], 1)
     t2r[:, me] = t2s[:, me]
+    send_frame(2)
+
+    def grad_last(n, carry):
+        at = pl.multiple_of(2304 + n * 256, 256)
+        dw[pl.ds(at, 256), :] = jnp.transpose(mm(gt[...], pat[:, pl.ds(at, 256)]))
+        return carry
+
+    lax.fori_loop(0, 4, grad_last, 0)
+    dw[3328:3456, :] = jnp.transpose(mm(gt[...], pat[:, 3328:3456]))
+    dw[3456:3464, :] = jnp.zeros((8, 256), F32)
+
+    to_partner(11, 16, 0)
 
     def grad_main(n, carry):
         at = pl.multiple_of(n * 256, 256)
@@ -315,7 +316,6 @@
         return carry
 
     lax.fori_loop(0, 3, grad_main, 0)
-    send_frame(2)
     send_frame(3)
     lax.fori_loop(3, 9, grad_main, 0)
 
@@ -349,7 +349,6 @@
             for p in range(2):
                 vs[p, k, t, 16:144, 0:128] = value[mine, 128 * p : 128 * p + 128]
 
-    stream_rows(1)
     z_copies = to_planes(11, 16, 0)
     landed(t2r.at[:, pl.ds(0, DEV - 1)], 1)
     loads[6].wait()
@@ -374,6 +373,7 @@
     to_partner(0, 11, 4)
 
 
+    stream_rows(1)
     stream_rows(2)
     stream_rows(3)
     def cell(k):
@@ -413,10 +413,11 @@
 
     z_copies += to_planes(0, 11, 4)
     stream_rows(0)
-    for k in range(3):
-        cell(k)
-        ship(k)
-    cell(3)
+    cell(0)
+    ship(0)
+    cell(1)
+    ship(1)
+    cell(2)
 
     for copy in z_copies:
         copy.wait()
@@ -429,6 +430,8 @@
         plane_copies.append(reduce_copy(s2b.at[other], r3.at[d - 1], 8, {"ctx": other * 2 + core}))
     for copy in plane_copies:
         copy.start()
+    ship(2)
+    cell(3)
     ship(3)
 
     pltpu.make_async_copy(r3, r3, red_recv.at[8]).wait()

time: 57.8 us -> 57.3 us (level); the launches traced: 56.7 us -> 57.1 us
  no operation moved by 1% of the time
where the time goes in v4:
time: 57.3 us; the launch traced here: 57.1 us
  Pallas kernels  56.5 us (99%)
  between operations  0.64 us (1%)
    pallas_call x1, Pallas kernels, per_device(): pl.pallas_call(section_kernel, out_shape=(jax.ShapeDtypeStruct((32, 4, 16...  53.8 us
    pallas_call x1, Pallas kernels, per_device(): pl.pallas_call(place_kernel, out_shape=(jax.ShapeDtypeStruct((4, 4, 128,...  2.72 us

profile of v4, /device:TPU:1, one launch (start us, length us, event | category | flops | bytes accessed | tf_op | source)
XLA Modules:
  0.0 57.1 jit_solution(2573842798254665915)
XLA Ops:
  0.6 53.8 %shard_map.149 = (bf16[32,4,16,256]{3,2,1,0:T(8,128)(2,1)}, f32[4,32,256]{2,1,0:T(8,128)}) custom-call(bf16[4,8,8,16,128]{4,3,2,1,0:T(8,128)(2,1)} %bitcast.4, bf16[3456,256]{1,0:T(8,128)(2,1)} %w_hbm.1, bf16[256,768]{1,0:T(8,128)(2,1)} %wqkv_hbm.1, bf16[256,256]{1,0:T(8,128)(2,1)} %wout_hbm.1, bf16[4,4,128,256]{3,2,1,0:T(8,128)(2,1)} %bitcast.5, ...), custom_call_target="tpu_custom_call" | custom-call | tf_op jit(solution)/shard_map/pallas_call | solution.py:526
  54.4 2.7 %shard_map.150 = (bf16[4,4,128,256]{3,2,1,0:T(8,128)(2,1)}, f32[108,256]{1,0:T(8,128)}) custom-call(bf16[32,4,16,256]{3,2,1,0:T(8,128)(2,1)} %get-tuple-element.6.back_ref, f32[4,32,256]{2,1,0:T(8,128)} %get-tuple-element.7.rows_ref, bf16[256,256]{1,0:T(8,128)(2,1)} %constant.17.clone.po_ref), custom_call_target="tpu_custom_call" | custom-call | tf_op jit(solution)/shard_map/pallas_call | solution.py:542

commit v5 on v4

--- a/solution.py
+++ b/solution.py
@@ -84,9 +84,10 @@
 
 
 def section_kernel(
-    x_hbm, w_hbm, wqkv_hbm, wout_hbm, ug_hbm, sa_ref, cnt_ref, scale_ref,
+    x_hbm, w_hbm, wqkv_hbm, wout_hbm, ug_hbm, sa_hbm, cnt_hbm, scale_hbm,
     px_hbm, pg_hbm, sh_hbm, ex_hbm, hs_hbm,
     back_ref, rows_ref,
+    sa_ref, cnt_ref, scale_ref,
     x_ref, px_ref, ug_ref, pg_ref, w_ref, ex_ref, sh_ref, wqkv_ref, hs_ref, wout_ref,
     xp, xt, pat, t1r, t2s, t2r, cs, cr, gt, dwt, dw, gf, gbs, r1, s1b, r2, acc2, s2b, r3, s4,
     hot_t, hot_s, hot_u, mask, ys, qs, ks, vs, osb, rb,
@@ -103,6 +104,7 @@
         for n, (source, target) in enumerate((
             (x_hbm, x_ref), (px_hbm, px_ref), (ug_hbm, ug_ref), (pg_hbm, pg_ref), (w_hbm, w_ref), (ex_hbm, ex_ref),
             (sh_hbm, sh_ref), (wqkv_hbm, wqkv_ref), (hs_hbm, hs_ref), (wout_hbm, wout_ref),
+            (sa_hbm, sa_ref), (cnt_hbm, cnt_ref), (scale_hbm, scale_ref),
         ))
     ]
     for load in loads[:2]:
@@ -244,6 +246,8 @@
     convolve(3)
     taps(0, False, (2,))
 
+    for load in loads[10:]:
+        load.wait()
     loads[5].wait()
     sa = sa_ref[...].astype(F32)
     opening = jnp.zeros((1, 128), jnp.bool_)
@@ -375,6 +379,7 @@
 
     stream_rows(1)
     stream_rows(2)
+    z_copies += to_planes(0, 11, 4)
     stream_rows(3)
     def cell(k):
         def tile(a, carry):
@@ -411,7 +416,6 @@
         spread(lambda peer: rb.at[k, peer], lambda mine: back_ref.at[mine, k], 6 + k)
         back_ref[me, k] = rb[k, me]
 
-    z_copies += to_planes(0, 11, 4)
     stream_rows(0)
     cell(0)
     ship(0)
@@ -474,6 +478,9 @@
 def per_device(pictures, slots, counts, scaling, taps, triple, final, upstream):
     vm = lambda shape, kind: pltpu.VMEM(shape, kind)
     scratch = [
+        vm((1, 128), jnp.int32),
+        pltpu.SMEM((16,), jnp.int32),
+        pltpu.SMEM((4,), F32),
         vm((4, 8, 8, 16, 128), BF),
         vm((384, 256), BF),
         vm((4, 4, 128, 256), BF),
@@ -518,10 +525,9 @@
         pltpu.SemaphoreType.DMA((10,)),
         pltpu.SemaphoreType.DMA((12,)),
         pltpu.SemaphoreType.DMA((12,)),
-        pltpu.SemaphoreType.DMA((10,)),
+        pltpu.SemaphoreType.DMA((13,)),
     ]
     v = pl.BlockSpec(memory_space=pltpu.VMEM)
-    s = pl.BlockSpec(memory_space=pltpu.SMEM)
     h = pl.BlockSpec(memory_space=pl.ANY)
     back, rows = pl.pallas_call(
         section_kernel,
@@ -529,7 +535,7 @@
             jax.ShapeDtypeStruct((32, 4, 16, 256), BF),
             jax.ShapeDtypeStruct((4, 32, 256), F32),
         ),
-        in_specs=[h, h, h, h, h, v, s, s, h, h, h, h, h],
+        in_specs=[h] * 13,
         out_specs=(v, v),
         scratch_shapes=scratch,
         compiler_params=pltpu.CompilerParams(

time: 57.3 us -> 55.7 us (0.972)
  Pallas kernels: 56.5 us -> 54.9 us
    pallas_call x1, Pallas kernels: 53.8 us -> 52.2 us  [per_device(): pl.pallas_call(section_kernel, out_shape=(jax.ShapeDtypeStruct((32, 4, 16...]
where the time goes in v5:
time: 55.7 us; the launch traced here: 55.5 us
  Pallas kernels  54.9 us (99%)
  between operations  0.64 us (1%)
    pallas_call x1, Pallas kernels, per_device(): pl.pallas_call(section_kernel, out_shape=(jax.ShapeDtypeStruct((32, 4, 16...  52.2 us
    pallas_call x1, Pallas kernels, per_device(): pl.pallas_call(place_kernel, out_shape=(jax.ShapeDtypeStruct((4, 4, 128,...  2.72 us

profile of v5, /device:TPU:1, one launch (start us, length us, event | category | flops | bytes accessed | tf_op | source)
XLA Modules:
  0.0 55.5 jit_solution(13931088332988406586)
XLA Ops:
  0.6 52.2 %shard_map.149 = (bf16[32,4,16,256]{3,2,1,0:T(8,128)(2,1)}, f32[4,32,256]{2,1,0:T(8,128)}) custom-call(bf16[4,8,8,16,128]{4,3,2,1,0:T(8,128)(2,1)} %bitcast.4, bf16[3456,256]{1,0:T(8,128)(2,1)} %w_hbm.1, bf16[256,768]{1,0:T(8,128)(2,1)} %wqkv_hbm.1, bf16[256,256]{1,0:T(8,128)(2,1)} %wout_hbm.1, bf16[4,4,128,256]{3,2,1,0:T(8,128)(2,1)} %bitcast.5, ...), custom_call_target="tpu_custom_call" | custom-call | tf_op jit(solution)/shard_map/pallas_call | solution.py:532
  52.8 2.7 %shard_map.150 = (bf16[4,4,128,256]{3,2,1,0:T(8,128)(2,1)}, f32[108,256]{1,0:T(8,128)}) custom-call(bf16[32,4,16,256]{3,2,1,0:T(8,128)(2,1)} %get-tuple-element.6.back_ref, f32[4,32,256]{2,1,0:T(8,128)} %get-tuple-element.7.rows_ref, bf16[256,256]{1,0:T(8,128)(2,1)} %constant.17.clone.po_ref), custom_call_target="tpu_custom_call" | custom-call | tf_op jit(solution)/shard_map/pallas_call | solution.py:548

commit v6 on v5

--- a/solution.py
+++ b/solution.py
@@ -308,7 +308,7 @@
         dw[pl.ds(at, 256), :] = jnp.transpose(mm(gt[...], pat[:, pl.ds(at, 256)]))
         return carry
 
-    lax.fori_loop(0, 4, grad_last, 0)
+    lax.fori_loop(0, 4, grad_last, 0, unroll=2)
     dw[3328:3456, :] = jnp.transpose(mm(gt[...], pat[:, 3328:3456]))
     dw[3456:3464, :] = jnp.zeros((8, 256), F32)
 
@@ -319,9 +319,9 @@
         dwt[:, pl.ds(at, 256)] = mm(gt[:, 512:2048], pat[512:2048, pl.ds(at, 256)])
         return carry
 
-    lax.fori_loop(0, 3, grad_main, 0)
+    lax.fori_loop(0, 3, grad_main, 0, unroll=3)
     send_frame(3)
-    lax.fori_loop(3, 9, grad_main, 0)
+    lax.fori_loop(3, 9, grad_main, 0, unroll=3)
 
     for load in loads[7:10]:
         load.wait()
@@ -465,7 +465,7 @@
 
 
 def place_kernel(back_ref, rows_ref, po_ref, out_ref, cg_ref):
-    for r in range(8):
+    for r in range(4):
         moved = mm(po_ref[...], back_ref[4 * r : 4 * r + 4].reshape(256, 256)).astype(BF)
         for s in range(4):
             for t in range(4):
@@ -551,8 +551,16 @@
             jax.ShapeDtypeStruct((4, 4, 128, 256), BF),
             jax.ShapeDtypeStruct((108, 256), F32),
         ),
-        in_specs=[v, v, v],
-        out_specs=(v, v),
+        grid=(2,),
+        in_specs=[
+            pl.BlockSpec((16, 4, 16, 256), lambda n: (n, 0, 0, 0)),
+            pl.BlockSpec((4, 32, 256), lambda n: (0, 0, 0)),
+            pl.BlockSpec((256, 256), lambda n: (0, 0)),
+        ],
+        out_specs=(
+            pl.BlockSpec((4, 4, 64, 256), lambda n: (0, 0, n, 0)),
+            pl.BlockSpec((108, 256), lambda n: (0, 0)),
+        ),
     )(back, rows, result_rows())
     return latents[None], conv_grad
 

time: 55.7 us -> 55.5 us (level)
  no operation moved by 1% of the time
where the time goes in v6:
time: 55.5 us; the launch traced here: 55.4 us
  Pallas kernels  54.8 us (99%)
  between operations  0.64 us (1%)
    pallas_call x1, Pallas kernels, per_device(): pl.pallas_call(section_kernel, out_shape=(jax.ShapeDtypeStruct((32, 4, 16...  52.1 us
    pallas_call x1, Pallas kernels, per_device(): pl.pallas_call(place_kernel, out_shape=(jax.ShapeDtypeStruct((4, 4, 128,...  2.6 us

profile of v6, /device:TPU:1, one launch (start us, length us, event | category | flops | bytes accessed | tf_op | source)
XLA Modules:
  0.0 55.4 jit_solution(12564187635954579337)
XLA Ops:
  0.6 52.1 %shard_map.149 = (bf16[32,4,16,256]{3,2,1,0:T(8,128)(2,1)}, f32[4,32,256]{2,1,0:T(8,128)}) custom-call(bf16[4,8,8,16,128]{4,3,2,1,0:T(8,128)(2,1)} %bitcast.4, bf16[3456,256]{1,0:T(8,128)(2,1)} %w_hbm.1, bf16[256,768]{1,0:T(8,128)(2,1)} %wqkv_hbm.1, bf16[256,256]{1,0:T(8,128)(2,1)} %wout_hbm.1, bf16[4,4,128,256]{3,2,1,0:T(8,128)(2,1)} %bitcast.5, ...), custom_call_target="tpu_custom_call" | custom-call | tf_op jit(solution)/shard_map/pallas_call | solution.py:532
  52.8 2.6 %shard_map.150 = (bf16[4,4,128,256]{3,2,1,0:T(8,128)(2,1)}, f32[108,256]{1,0:T(8,128)}) custom-call(bf16[32,4,16,256]{3,2,1,0:T(8,128)(2,1)} %get-tuple-element.6.back_ref, f32[4,32,256]{2,1,0:T(8,128)} %get-tuple-element.7.rows_ref, bf16[256,256]{1,0:T(8,128)(2,1)} %constant.17.clone.po_ref), custom_call_target="tpu_custom_call" | custom-call | tf_op jit(solution)/shard_map/pallas_call | solution.py:548
